TPU v7x, 256 devices: a whole 4x4x8 slice. The times are simulated.
256 devices in a mesh: pert: 8 (over z_lo, y), space: 32 (over x, z_hi, core).
Axes of the slice: x: 4, y: 4, z: 8 (z_hi: 4, z_lo: 2; z = z_hi * 2 + z_lo), core: 2. Of those that a mesh axis runs over, the one named last changes fastest.
Arguments:
- spectra: float32 [320, 320, 1024], P('space', None, 'pert'), may hold values from -6 to 6
- wave_order: int32 [320], replicated, may hold values from 0 to 319, as said below
- traj_wind: bfloat16 [2, 32, 480, 960], P(None, 'pert', 'space'), may hold values from -0.029907227 to 0.029907227
- traj_state: bfloat16 [2, 2, 32, 480, 960], P(None, None, 'pert', 'space'), may hold values from -6 to 6
- vertical_modes: float32 [32, 32], replicated, may hold values from -0.75 to 0.75
- mode_speeds: float32 [32], replicated, may hold values from 1e-06 to 0.001
Outputs:
- spectra_out: float32 [320, 320, 1024], P('space', None, 'pert')
Inputs may be any that keep to these rules, and one draw needn't show every extreme that they name: wave_order is a permutation of 0 to 319 in which slots 2 i and 2 i + 1 hold two wavenumbers that add up to 319.
All inputs are finite; a program needn't handle non-finite values.
Results may differ from a plain program's by a relative error of at most 0.0085.
Values may be sent and summed in bfloat16 or wider, within the bound.
A program may use at most 128 MiB of HBM per device.

v0:
```python
import math

import jax
import jax.numpy as jnp
from jax import lax
from jax.sharding import PartitionSpec as P

NLAT = 480
NLON = 960
M = 320
VARS = 2
LEV = 32
STEPS = 2


def grid_angles():
    colatitude = (jnp.arange(NLAT, dtype=jnp.float32) + 0.5) * (math.pi / NLAT)
    return (jnp.cos(colatitude), jnp.sin(colatitude))


def sectoral_log(wave_float, sine_values):
    gammas = jax.scipy.special.gammaln
    start = 0.5 * (
        gammas(wave_float + 1.5) - gammas(wave_float + 1.0) - gammas(jnp.float32(1.5))
    ) - 0.5 * math.log(2.0)
    return start[:, None] + wave_float[:, None] * jnp.log(sine_values)[None, :]


def coefficient(wave_float, degree):
    return jnp.sqrt((4.0 * degree * degree - 1.0) / ((degree - wave_float) * (degree + wave_float)))


def legendre_local(wave_list):
    cosines, sine_values = grid_angles()
    slot_count = wave_list.shape[0]
    block_count = M // 16
    wave_float = wave_list.astype(jnp.float32)[:, None, None]
    cos_row = cosines[None, None, :]
    block_start = (jnp.arange(block_count, dtype=jnp.int32) * 16)[None, :, None]

    def matrix_at(offset):
        degree_offset = block_start + offset
        offset_float = degree_offset.astype(jnp.float32)
        safe_one = wave_float + jnp.maximum(offset_float, 1.0)
        safe_two = wave_float + jnp.maximum(offset_float, 2.0)
        upper_coef = coefficient(wave_float, safe_one)
        lower_coef = coefficient(wave_float, safe_two - 1.0)
        first_row = jnp.where(degree_offset == 0, 1.0, upper_coef * cos_row)
        corner = jnp.where(degree_offset >= 2, -upper_coef / lower_coef, 0.0)
        lower_left = jnp.where(degree_offset == 0, 0.0, 1.0)
        lower_right = jnp.where(degree_offset == 0, 1.0, 0.0)
        return (first_row, corner, lower_left, lower_right)

    block_shape = (slot_count, block_count, NLAT)
    unit_block = jnp.ones(block_shape, jnp.float32)
    zero_block = jnp.zeros(block_shape, jnp.float32)

    def grow_block(offset, loop_carry):
        top_left, top_right, low_left, low_right = loop_carry
        first_row, corner, lower_left, lower_right = matrix_at(offset)
        return (
            first_row * top_left + corner * low_left,
            first_row * top_right + corner * low_right,
            lower_left * top_left + lower_right * low_left,
            lower_left * top_right + lower_right * low_right,
        )

    product = lax.fori_loop(0, 16, grow_block, (unit_block, zero_block, zero_block, unit_block))

    def chain_blocks(loop_carry, entries):
        head_value, tail_value, log_scale = loop_carry
        top_left, top_right, low_left, low_right = entries
        new_head = top_left * head_value + top_right * tail_value
        new_tail = low_left * head_value + low_right * tail_value
        biggest = jnp.maximum(jnp.abs(new_head), jnp.abs(new_tail))
        return (
            (new_head / biggest, new_tail / biggest, log_scale + jnp.log(biggest)),
            (head_value, tail_value, log_scale),
        )

    first_state = (
        jnp.ones((slot_count, NLAT), jnp.float32),
        jnp.zeros((slot_count, NLAT), jnp.float32),
        jnp.zeros((slot_count, NLAT), jnp.float32),
    )
    final_state, starts = lax.scan(
        chain_blocks, first_state, tuple((jnp.moveaxis(entry, 1, 0) for entry in product))
    )
    head_all = jnp.moveaxis(starts[0], 0, 1)
    tail_all = jnp.moveaxis(starts[1], 0, 1)
    scale_all = jnp.moveaxis(starts[2], 0, 1)
    start_scale = jnp.exp(
        sectoral_log(wave_list.astype(jnp.float32), sine_values)[:, None, :] + scale_all
    )

    def unfold(loop_carry, offset):
        head_value, tail_value = loop_carry
        first_row, corner, lower_left, lower_right = matrix_at(offset)
        new_head = first_row * head_value + corner * tail_value
        new_tail = lower_left * head_value + lower_right * tail_value
        return ((new_head, new_tail), new_head * start_scale)

    final_loop, table_rows = lax.scan(unfold, (head_all, tail_all), jnp.arange(16, dtype=jnp.int32))
    legendre = jnp.transpose(table_rows, (1, 2, 0, 3)).reshape(slot_count, M, NLAT)
    inside = wave_list[:, None] + jnp.arange(M, dtype=jnp.int32)[None, :] <= M - 1
    return legendre * inside[:, :, None].astype(jnp.float32)


def zonal_tables(wave_list):
    cell_index = jnp.arange(NLON, dtype=jnp.int32)
    phase_index = wave_list[:, None] * cell_index[None, :] % NLON
    angles = phase_index.astype(jnp.float32) * (2.0 * math.pi / NLON)
    factor = jnp.where(wave_list == 0, 1.0, 2.0).astype(jnp.float32)[:, None]
    synth_table = jnp.stack([factor * jnp.cos(angles), -factor * jnp.sin(angles)]).astype(
        jnp.bfloat16
    )
    analysis = (jnp.stack([jnp.cos(angles).T, -jnp.sin(angles).T], axis=1) / NLON).astype(
        jnp.bfloat16
    )
    return (synth_table, analysis)


def spectral_mask(wave_list, columns):
    degree_offset = jnp.arange(M, dtype=jnp.int32)
    inside = wave_list[:, None] + degree_offset[None, :] <= M - 1
    imaginary = jnp.arange(columns, dtype=jnp.int32) % 2 == 1
    dropped = (wave_list[:, None] == 0) & imaginary[None, :]
    return (inside[:, :, None] & jnp.logical_not(dropped)[:, None, :]).astype(jnp.float32)


def vertical_operators(wave_list, vertical_modes, mode_speeds, columns):
    degree = (wave_list[:, None] + jnp.arange(M, dtype=jnp.int32)[None, :]).astype(jnp.float32)
    stiffness = mode_speeds[None, None, :] * (degree * (degree + 1.0))[:, :, None]
    damping = stiffness / (1.0 + stiffness)
    column = jnp.arange(columns, dtype=jnp.int32)
    onehot = ((column // 2 % LEV)[:, None] == jnp.arange(LEV, dtype=jnp.int32)[None, :]).astype(
        jnp.float32
    )
    column_group = column // (2 * LEV) * 2 + column % 2
    same_group = (column_group[:, None] == column_group[None, :]).astype(jnp.float32)
    spread = jnp.dot(onehot, vertical_modes.T, precision=lax.Precision.HIGHEST)
    mixing = jnp.dot(spread, onehot.T, precision=lax.Precision.HIGHEST) * same_group
    damping_cols = jnp.dot(damping, onehot.T, precision=lax.Precision.HIGHEST)
    return (damping_cols, mixing)


def implicit_update(spectral_state, change, damping_cols, mixing, keep_mask):
    combined = spectral_state + change
    projected = jnp.dot(combined, mixing, precision=lax.Precision.HIGHEST)
    returned = jnp.dot(damping_cols * projected, mixing.T, precision=lax.Precision.HIGHEST)
    return (combined - returned) * keep_mask


def zonal_slope(fourier, wave_list):
    part_pairs = fourier.reshape(fourier.shape[:-1] + (fourier.shape[-1] // 2, 2)).astype(
        jnp.float32
    )
    factor = wave_list.astype(jnp.float32).reshape((-1,) + (1,) * (part_pairs.ndim - 1))
    turned = jnp.stack([-part_pairs[..., 1], part_pairs[..., 0]], axis=-1) * factor
    return turned.reshape(fourier.shape).astype(jnp.bfloat16)


def synthesis(fourier, synth_table):
    part_pairs = fourier.reshape(fourier.shape[0], fourier.shape[1], -1, 2)
    return jnp.einsum("jtrc,cjx->trx", part_pairs, synth_table, preferred_element_type=jnp.float32)


def tendency(grid_values, grid_slopes, wind_now, traj_now):
    lat_count = grid_values.shape[0]
    shaped = (lat_count, -1, VARS, LEV, NLON)
    values_five = grid_values.reshape(shaped)
    slopes_five = grid_slopes.reshape(shaped)
    wind_rows = jnp.transpose(wind_now, (1, 0, 2)).astype(jnp.float32)[:, None, None, :, :]
    state_rows = jnp.roll(jnp.transpose(traj_now, (2, 0, 1, 3)), -1, axis=1).astype(jnp.float32)[
        :, None
    ]
    shifted = jnp.roll(values_five, -2, axis=2)
    forcing = -wind_rows * slopes_five - state_rows * shifted
    return forcing.reshape(lat_count, -1, NLON).astype(jnp.bfloat16)


def analysis_step(forcing, analysis):
    lat_count = forcing.shape[0]
    fourier = jnp.einsum("trx,xcj->jtrc", forcing, analysis, preferred_element_type=jnp.float32)
    return fourier.astype(jnp.bfloat16).reshape(analysis.shape[2], lat_count, -1)


def shards(spectra, wave_order, traj_wind, traj_state, vertical_modes, mode_speeds):
    slots_here = spectra.shape[0]
    columns = spectra.shape[2]
    first_slot = lax.axis_index("space") * slots_here
    wave_here = lax.dynamic_slice_in_dim(wave_order, first_slot, slots_here)
    legendre = legendre_local(wave_here)
    angle_pair = grid_angles()
    inverse_table = legendre.astype(jnp.bfloat16)
    forward_table = (legendre * (angle_pair[1] * (math.pi / NLAT))[None, None, :]).astype(
        jnp.bfloat16
    )
    synth_table, analysis = zonal_tables(wave_order)
    keep_mask = spectral_mask(wave_here, columns)
    damping_cols, mixing = vertical_operators(wave_here, vertical_modes, mode_speeds, columns)
    spectral_state = spectra * keep_mask
    for step_idx in range(STEPS):
        wind_now, traj_now = (
            lax.all_gather(traj_wind[step_idx], "pert", axis=0, tiled=True),
            lax.all_gather(traj_state[step_idx], "pert", axis=1, tiled=True),
        )
        fourier_rows = jnp.einsum(
            "jkt,jkc->jtc",
            inverse_table,
            spectral_state.astype(jnp.bfloat16),
            preferred_element_type=jnp.float32,
        ).astype(jnp.bfloat16)
        slope_rows = zonal_slope(fourier_rows, wave_here)
        fourier, fourier_slope = (
            lax.all_to_all(fourier_rows, "space", split_axis=1, concat_axis=0, tiled=True),
            lax.all_to_all(slope_rows, "space", split_axis=1, concat_axis=0, tiled=True),
        )
        grid_values = synthesis(fourier, synth_table)
        grid_slopes = synthesis(fourier_slope, synth_table)
        forcing = tendency(grid_values, grid_slopes, wind_now, traj_now)
        wave_lat = analysis_step(forcing, analysis)
        wave_rows = lax.all_to_all(wave_lat, "space", split_axis=0, concat_axis=1, tiled=True)
        change = jnp.einsum(
            "jkt,jtc->jkc", forward_table, wave_rows, preferred_element_type=jnp.float32
        )
        spectral_state = implicit_update(spectral_state, change, damping_cols, mixing, keep_mask)
    return spectral_state


def solution(mesh):
    placed = (
        P("space", None, "pert"),
        P(),
        P(None, "pert", "space", None),
        P(None, None, "pert", "space", None),
        P(),
        P(),
    )
    return jax.shard_map(
        shards, mesh=mesh, in_specs=placed, out_specs=P("space", None, "pert"), check_vma=False
    )
```

profile of v0, /device:TPU:1, one launch (start us, length us, event | category | flops | bytes accessed | tf_op | source)
XLA Modules:
  0.0 1074.4 jit_solution(18004682437190741774)
XLA Ops:
  7.6 13.6 %while.63 = (s32[]{:T(128)}, f32[10,20,480]{2,1,0:T(8,128)S(1)}, f32[10,20,480]{2,1,0:T(8,128)S(1)}, f32[10,20,480]{2,1,0:T(8,128)S(1)}, f32[10,20,480]{2,1,0:T(...) while((s32[]{:T(128)}, f32[10,20,480]{2,1,0:T(8,128)S(1)}, ...), condition=%wide.region_1.2_spmd.clone, body=%wide.region_0.1_spmd.clone.sunk | while | flops 1733243 | bytes 3079907 | solution.py:68
  23.1 41.6 %while.64 = (s32[]{:T(128)}, f32[10,480]{1,0:T(8,128)S(1)}, f32[10,480]{1,0:T(8,128)S(1)}, f32[10,480]{1,0:T(8,128)S(1)}, f32[20,10,480]{2,1,0:T(8,128)}, /*inde...) while((s32[]{:T(128)}, f32[10,480]{1,0:T(8,128)S(1)}, ...), condition=%wide.region_3.4_spmd.clone, body=%wide.region_2.3_spmd.clone.sunk | while | flops 100803 | bytes 425869 | solution.py:86
  66.8 278.1 %while.62 = (s32[]{:T(128)}, f32[10,20,480]{2,1,0:T(8,128)S(1)}, f32[10,20,480]{2,1,0:T(8,128)S(1)}, f32[16,10,20,480]{3,0,2,1:T(8,128)}, s32[16]{0:T(128)S(1)},...) while((s32[]{:T(128)}, f32[10,20,480]{2,1,0:T(8,128)S(1)}, ...), condition=%wide.region_5.6_spmd.clone, body=%wide.region_4.5_spmd.clone.sunk | while | flops 869242 | bytes 3847921 | solution.py:103
  70.3 13.9 %dynamic_update_slice.28 = f32[16,10,20,480]{3,0,2,1:T(8,128)} dynamic-update-slice(f32[16,10,20,480]{3,0,2,1:T(8,128)} %get-tuple-element.927, f32[1,10,20,480]{3,0,2,1:T(1,128)S(1)} %copy.137, s32[]{:T(128)} %get-tuple-element.924, s32[]{:T(128)} %constant.294.clone.1..sunk, s32[]{:T(128)} %constant.294.clone.1..sunk, s32[]{:T(128)} %constant.294.clone.1..sunk) | dynamic-update-slice | bytes 768004 | tf_op jit(solution)/shard_map/while/body/jit(dynamic_update_index_in_dim)/dynamic_update_slice | solution.py:103
  87.7 13.9 %dynamic_update_slice.28 = f32[16,10,20,480]{3,0,2,1:T(8,128)} dynamic-update-slice(f32[16,10,20,480]{3,0,2,1:T(8,128)} %get-tuple-element.927, f32[1,10,20,480]{3,0,2,1:T(1,128)S(1)} %copy.137, s32[]{:T(128)} %get-tuple-element.924, s32[]{:T(128)} %constant.294.clone.1..sunk, s32[]{:T(128)} %constant.294.clone.1..sunk, s32[]{:T(128)} %constant.294.clone.1..sunk) | dynamic-update-slice | bytes 768004 | tf_op jit(solution)/shard_map/while/body/jit(dynamic_update_index_in_dim)/dynamic_update_slice | solution.py:103
  105.1 13.9 %dynamic_update_slice.28 = f32[16,10,20,480]{3,0,2,1:T(8,128)} dynamic-update-slice(f32[16,10,20,480]{3,0,2,1:T(8,128)} %get-tuple-element.927, f32[1,10,20,480]{3,0,2,1:T(1,128)S(1)} %copy.137, s32[]{:T(128)} %get-tuple-element.924, s32[]{:T(128)} %constant.294.clone.1..sunk, s32[]{:T(128)} %constant.294.clone.1..sunk, s32[]{:T(128)} %constant.294.clone.1..sunk) | dynamic-update-slice | bytes 768004 | tf_op jit(solution)/shard_map/while/body/jit(dynamic_update_index_in_dim)/dynamic_update_slice | solution.py:103
  122.5 13.9 %dynamic_update_slice.28 = f32[16,10,20,480]{3,0,2,1:T(8,128)} dynamic-update-slice(f32[16,10,20,480]{3,0,2,1:T(8,128)} %get-tuple-element.927, f32[1,10,20,480]{3,0,2,1:T(1,128)S(1)} %copy.137, s32[]{:T(128)} %get-tuple-element.924, s32[]{:T(128)} %constant.294.clone.1..sunk, s32[]{:T(128)} %constant.294.clone.1..sunk, s32[]{:T(128)} %constant.294.clone.1..sunk) | dynamic-update-slice | bytes 768004 | tf_op jit(solution)/shard_map/while/body/jit(dynamic_update_index_in_dim)/dynamic_update_slice | solution.py:103
  139.8 13.9 %dynamic_update_slice.28 = f32[16,10,20,480]{3,0,2,1:T(8,128)} dynamic-update-slice(f32[16,10,20,480]{3,0,2,1:T(8,128)} %get-tuple-element.927, f32[1,10,20,480]{3,0,2,1:T(1,128)S(1)} %copy.137, s32[]{:T(128)} %get-tuple-element.924, s32[]{:T(128)} %constant.294.clone.1..sunk, s32[]{:T(128)} %constant.294.clone.1..sunk, s32[]{:T(128)} %constant.294.clone.1..sunk) | dynamic-update-slice | bytes 768004 | tf_op jit(solution)/shard_map/while/body/jit(dynamic_update_index_in_dim)/dynamic_update_slice | solution.py:103
  157.2 13.9 %dynamic_update_slice.28 = f32[16,10,20,480]{3,0,2,1:T(8,128)} dynamic-update-slice(f32[16,10,20,480]{3,0,2,1:T(8,128)} %get-tuple-element.927, f32[1,10,20,480]{3,0,2,1:T(1,128)S(1)} %copy.137, s32[]{:T(128)} %get-tuple-element.924, s32[]{:T(128)} %constant.294.clone.1..sunk, s32[]{:T(128)} %constant.294.clone.1..sunk, s32[]{:T(128)} %constant.294.clone.1..sunk) | dynamic-update-slice | bytes 768004 | tf_op jit(solution)/shard_map/while/body/jit(dynamic_update_index_in_dim)/dynamic_update_slice | solution.py:103
  174.6 13.9 %dynamic_update_slice.28 = f32[16,10,20,480]{3,0,2,1:T(8,128)} dynamic-update-slice(f32[16,10,20,480]{3,0,2,1:T(8,128)} %get-tuple-element.927, f32[1,10,20,480]{3,0,2,1:T(1,128)S(1)} %copy.137, s32[]{:T(128)} %get-tuple-element.924, s32[]{:T(128)} %constant.294.clone.1..sunk, s32[]{:T(128)} %constant.294.clone.1..sunk, s32[]{:T(128)} %constant.294.clone.1..sunk) | dynamic-update-slice | bytes 768004 | tf_op jit(solution)/shard_map/while/body/jit(dynamic_update_index_in_dim)/dynamic_update_slice | solution.py:103
  192.0 13.9 %dynamic_update_slice.28 = f32[16,10,20,480]{3,0,2,1:T(8,128)} dynamic-update-slice(f32[16,10,20,480]{3,0,2,1:T(8,128)} %get-tuple-element.927, f32[1,10,20,480]{3,0,2,1:T(1,128)S(1)} %copy.137, s32[]{:T(128)} %get-tuple-element.924, s32[]{:T(128)} %constant.294.clone.1..sunk, s32[]{:T(128)} %constant.294.clone.1..sunk, s32[]{:T(128)} %constant.294.clone.1..sunk) | dynamic-update-slice | bytes 768004 | tf_op jit(solution)/shard_map/while/body/jit(dynamic_update_index_in_dim)/dynamic_update_slice | solution.py:103
  209.4 13.9 %dynamic_update_slice.28 = f32[16,10,20,480]{3,0,2,1:T(8,128)} dynamic-update-slice(f32[16,10,20,480]{3,0,2,1:T(8,128)} %get-tuple-element.927, f32[1,10,20,480]{3,0,2,1:T(1,128)S(1)} %copy.137, s32[]{:T(128)} %get-tuple-element.924, s32[]{:T(128)} %constant.294.clone.1..sunk, s32[]{:T(128)} %constant.294.clone.1..sunk, s32[]{:T(128)} %constant.294.clone.1..sunk) | dynamic-update-slice | bytes 768004 | tf_op jit(solution)/shard_map/while/body/jit(dynamic_update_index_in_dim)/dynamic_update_slice | solution.py:103
  226.8 13.9 %dynamic_update_slice.28 = f32[16,10,20,480]{3,0,2,1:T(8,128)} dynamic-update-slice(f32[16,10,20,480]{3,0,2,1:T(8,128)} %get-tuple-element.927, f32[1,10,20,480]{3,0,2,1:T(1,128)S(1)} %copy.137, s32[]{:T(128)} %get-tuple-element.924, s32[]{:T(128)} %constant.294.clone.1..sunk, s32[]{:T(128)} %constant.294.clone.1..sunk, s32[]{:T(128)} %constant.294.clone.1..sunk) | dynamic-update-slice | bytes 768004 | tf_op jit(solution)/shard_map/while/body/jit(dynamic_update_index_in_dim)/dynamic_update_slice | solution.py:103
  244.1 13.9 %dynamic_update_slice.28 = f32[16,10,20,480]{3,0,2,1:T(8,128)} dynamic-update-slice(f32[16,10,20,480]{3,0,2,1:T(8,128)} %get-tuple-element.927, f32[1,10,20,480]{3,0,2,1:T(1,128)S(1)} %copy.137, s32[]{:T(128)} %get-tuple-element.924, s32[]{:T(128)} %constant.294.clone.1..sunk, s32[]{:T(128)} %constant.294.clone.1..sunk, s32[]{:T(128)} %constant.294.clone.1..sunk) | dynamic-update-slice | bytes 768004 | tf_op jit(solution)/shard_map/while/body/jit(dynamic_update_index_in_dim)/dynamic_update_slice | solution.py:103
  261.5 13.9 %dynamic_update_slice.28 = f32[16,10,20,480]{3,0,2,1:T(8,128)} dynamic-update-slice(f32[16,10,20,480]{3,0,2,1:T(8,128)} %get-tuple-element.927, f32[1,10,20,480]{3,0,2,1:T(1,128)S(1)} %copy.137, s32[]{:T(128)} %get-tuple-element.924, s32[]{:T(128)} %constant.294.clone.1..sunk, s32[]{:T(128)} %constant.294.clone.1..sunk, s32[]{:T(128)} %constant.294.clone.1..sunk) | dynamic-update-slice | bytes 768004 | tf_op jit(solution)/shard_map/while/body/jit(dynamic_update_index_in_dim)/dynamic_update_slice | solution.py:103
  278.9 13.9 %dynamic_update_slice.28 = f32[16,10,20,480]{3,0,2,1:T(8,128)} dynamic-update-slice(f32[16,10,20,480]{3,0,2,1:T(8,128)} %get-tuple-element.927, f32[1,10,20,480]{3,0,2,1:T(1,128)S(1)} %copy.137, s32[]{:T(128)} %get-tuple-element.924, s32[]{:T(128)} %constant.294.clone.1..sunk, s32[]{:T(128)} %constant.294.clone.1..sunk, s32[]{:T(128)} %constant.294.clone.1..sunk) | dynamic-update-slice | bytes 768004 | tf_op jit(solution)/shard_map/while/body/jit(dynamic_update_index_in_dim)/dynamic_update_slice | solution.py:103
  296.3 13.9 %dynamic_update_slice.28 = f32[16,10,20,480]{3,0,2,1:T(8,128)} dynamic-update-slice(f32[16,10,20,480]{3,0,2,1:T(8,128)} %get-tuple-element.927, f32[1,10,20,480]{3,0,2,1:T(1,128)S(1)} %copy.137, s32[]{:T(128)} %get-tuple-element.924, s32[]{:T(128)} %constant.294.clone.1..sunk, s32[]{:T(128)} %constant.294.clone.1..sunk, s32[]{:T(128)} %constant.294.clone.1..sunk) | dynamic-update-slice | bytes 768004 | tf_op jit(solution)/shard_map/while/body/jit(dynamic_update_index_in_dim)/dynamic_update_slice | solution.py:103
  313.6 13.9 %dynamic_update_slice.28 = f32[16,10,20,480]{3,0,2,1:T(8,128)} dynamic-update-slice(f32[16,10,20,480]{3,0,2,1:T(8,128)} %get-tuple-element.927, f32[1,10,20,480]{3,0,2,1:T(1,128)S(1)} %copy.137, s32[]{:T(128)} %get-tuple-element.924, s32[]{:T(128)} %constant.294.clone.1..sunk, s32[]{:T(128)} %constant.294.clone.1..sunk, s32[]{:T(128)} %constant.294.clone.1..sunk) | dynamic-update-slice | bytes 768004 | tf_op jit(solution)/shard_map/while/body/jit(dynamic_update_index_in_dim)/dynamic_update_slice | solution.py:103
  331.0 13.9 %dynamic_update_slice.28 = f32[16,10,20,480]{3,0,2,1:T(8,128)} dynamic-update-slice(f32[16,10,20,480]{3,0,2,1:T(8,128)} %get-tuple-element.927, f32[1,10,20,480]{3,0,2,1:T(1,128)S(1)} %copy.137, s32[]{:T(128)} %get-tuple-element.924, s32[]{:T(128)} %constant.294.clone.1..sunk, s32[]{:T(128)} %constant.294.clone.1..sunk, s32[]{:T(128)} %constant.294.clone.1..sunk) | dynamic-update-slice | bytes 768004 | tf_op jit(solution)/shard_map/while/body/jit(dynamic_update_index_in_dim)/dynamic_update_slice | solution.py:103
  345.0 3.5 fusion.30
  350.1 2.9 convolution_convert_fusion.3
  355.9 4.7 reshape.1193
  360.5 5.3 slice_negate_fusion.1
  365.9 3.9 pad_maximum_fusion
  369.8 4.6 stack.25
  374.4 3.2 multiply_convert_fusion.2
  377.6 4.3 copy.59
  381.9 12.6 %all-to-all-start = ((bf16[10,480,128]{2,0,1:T(8,128)(2,1)}), bf16[10,480,128]{2,0,1:T(8,128)(2,1)}, u32[]{:S(2)}, u32[]{:S(2)}) async-start(bf16[10,480,128]{2,0,1:T(8,128)(2,1)} %copy.59), calls=%async_computation | async-start | bytes 3932160 | tf_op jit(solution)/shard_map/all_to_all | solution.py:217
  397.4 3.1 copy.66
  400.6 56.8 %all-to-all-done = bf16[10,480,128]{2,0,1:T(8,128)(2,1)} async-done(((bf16[10,480,128]{2,0,1:T(8,128)(2,1)}), bf16[10,480,128]{2,0,1:T(8,128)(2,1)}, u32[]{:S(2)}, u32[]{:S(2)}) %all-to-all-start) | async-done | bytes 1228832 | tf_op jit(solution)/shard_map/all_to_all | solution.py:217
  457.3 5.0 all-to-all-start.1
  463.4 63.7 %all-gather = bf16[1,32,15,960]{3,2,0,1:T(8,128)(2,1)S(1)} all-gather(bf16[1,4,15,960]{3,2,0,1:T(8,128)(2,1)S(1)} %copy.116), channel_id=2, replica_groups=mesh['pert'=8,'space'=32] {'pert'}, dimensions={1}, use_global_device_ids=true | all-gather | bytes 1036800 | tf_op jit(solution)/shard_map/all_gather | solution.py:205
  529.8 7.3 multiply_convert_fusion.4
  537.1 7.3 fusion.62
  544.4 13.0 %copy.61 = bf16[32,10,15,128]{1,0,3,2:T(8,128)(2,1)} copy(bf16[32,10,15,128]{3,1,2,0:T(8,128)(2,1)} %bitcast.16) | data formatting | bytes 2457600 | tf_op jit(solution)/shard_map/all_to_all | solution.py:217
  557.4 31.3 %reshape.1187 = bf16[320,15,64,2]{0,3,2,1:T(2,128)(2,1)} reshape(bf16[32,10,15,128]{1,0,3,2:T(8,128)(2,1)} %copy.61) | data formatting | bytes 2457600 | tf_op jit(solution)/shard_map/reshape | solution.py:164
  588.7 13.0 %copy.68 = bf16[32,10,15,128]{1,0,3,2:T(8,128)(2,1)} copy(bf16[32,10,15,128]{3,1,2,0:T(8,128)(2,1)} %bitcast.28) | data formatting | bytes 2457600 | tf_op jit(solution)/shard_map/all_to_all | solution.py:216
  601.7 31.3 %reshape.1188 = bf16[320,15,64,2]{0,3,2,1:T(2,128)(2,1)} reshape(bf16[32,10,15,128]{1,0,3,2:T(8,128)(2,1)} %copy.68) | data formatting | bytes 2457600 | tf_op jit(solution)/shard_map/reshape | solution.py:164
  633.0 5.3 fusion.48
  642.5 4.4 fusion.34
  651.3 4.4 reshape.1189
  658.6 15.6 %all-to-all-start.2 = ((bf16[320,15,128]{2,1,0:T(8,128)(2,1)}), bf16[320,15,128]{2,1,0:T(8,128)(2,1)}, u32[]{:S(2)}, u32[]{:S(2)}) async-start(bf16[320,15,128]{2,1,0:T(8,128)(2,1)} %copy.72), calls=%async_computation.2 | async-start | bytes 2621440 | tf_op jit(solution)/shard_map/all_to_all | solution.py:223
  677.5 27.5 %all-to-all-done.2 = bf16[320,15,128]{2,1,0:T(8,128)(2,1)} async-done(((bf16[320,15,128]{2,1,0:T(8,128)(2,1)}), bf16[320,15,128]{2,1,0:T(8,128)(2,1)}, u32[]{:S(2)}, u32[]{:S(2)}) %all-to-all-start.2) | async-done | bytes 1228832 | tf_op jit(solution)/shard_map/all_to_all | solution.py:223
  707.7 3.2 all_to_all.79
  723.2 4.7 reshape.1194
  727.9 5.3 slice_negate_fusion
  733.2 3.9 pad_maximum_fusion.1
  737.2 4.6 stack.28
  741.8 3.2 multiply_convert_fusion.1
  745.0 4.3 copy.77
  749.2 8.0 all-to-all-start.3
  759.2 3.1 copy.84
  762.3 55.8 %all-to-all-done.3 = bf16[10,480,128]{2,0,1:T(8,128)(2,1)} async-done(((bf16[10,480,128]{2,0,1:T(8,128)(2,1)}), bf16[10,480,128]{2,0,1:T(8,128)(2,1)}, u32[]{:S(2)}, u32[]{:S(2)}) %all-to-all-start.3) | async-done | bytes 1228832 | tf_op jit(solution)/shard_map/all_to_all | solution.py:217
  818.1 6.0 all-to-all-start.4
  824.1 63.0 %all-gather.2 = bf16[1,32,15,960]{3,2,0,1:T(8,128)(2,1)S(1)} all-gather(bf16[1,4,15,960]{3,2,0,1:T(8,128)(2,1)S(1)} %copy.118), channel_id=4, replica_groups=mesh['pert'=8,'space'=32] {'pert'}, dimensions={1}, use_global_device_ids=true | all-gather | bytes 1036800 | tf_op jit(solution)/shard_map/all_gather | solution.py:205
  893.5 13.2 %copy.79 = bf16[32,10,15,128]{1,0,3,2:T(8,128)(2,1)} copy(bf16[32,10,15,128]{3,1,2,0:T(8,128)(2,1)} %bitcast.46) | data formatting | bytes 2457600 | tf_op jit(solution)/shard_map/all_to_all | solution.py:217
  906.6 31.3 %reshape.1190 = bf16[320,15,64,2]{0,3,2,1:T(2,128)(2,1)} reshape(bf16[32,10,15,128]{1,0,3,2:T(8,128)(2,1)} %copy.79) | data formatting | bytes 2457600 | tf_op jit(solution)/shard_map/reshape | solution.py:164
  937.9 5.3 fusion.45
  943.2 13.0 %copy.86 = bf16[32,10,15,128]{1,0,3,2:T(8,128)(2,1)} copy(bf16[32,10,15,128]{3,1,2,0:T(8,128)(2,1)} %bitcast.56) | data formatting | bytes 2457600 | tf_op jit(solution)/shard_map/all_to_all | solution.py:216
  956.2 31.3 %reshape.1191 = bf16[320,15,64,2]{0,3,2,1:T(2,128)(2,1)} reshape(bf16[32,10,15,128]{1,0,3,2:T(8,128)(2,1)} %copy.86) | data formatting | bytes 2457600 | tf_op jit(solution)/shard_map/reshape | solution.py:164
  987.5 6.1 fusion.32
  998.0 4.7 reshape.1192
  1005.5 50.1 %all_to_all.96 = bf16[320,15,128]{2,1,0:T(8,128)(2,1)S(1)} all-to-all(bf16[320,15,128]{2,1,0:T(8,128)(2,1)} %copy.90), channel_id=1, replica_groups=mesh['pert'=8,'space'=32] {'space'}, dimensions={0} | all-to-all | bytes 2457600 | tf_op jit(solution)/shard_map/all_to_all | solution.py:223
  1057.0 3.2 all_to_all.89
  (416 shorter events, 178.1 us)
Async XLA Ops:
  6.5 667.7 %copy-start = (f32[32,32]{1,0:T(8,128)S(1)}, f32[32,32]{1,0:T(8,128)}, u32[]{:S(2)}) copy-start(f32[32,32]{1,0:T(8,128)} %param.16) | copy-start | bytes 12292
  64.7 1.6 copy-start.16
  64.8 1.8 copy-start.17
  345.0 5.2 copy-start.5
  348.5 1.7 copy-start.2
  381.9 75.4 %all-to-all-start = ((bf16[10,480,128]{2,0,1:T(8,128)(2,1)}), bf16[10,480,128]{2,0,1:T(8,128)(2,1)}, u32[]{:S(2)}, u32[]{:S(2)}) async-start(bf16[10,480,128]{2,0,1:T(8,128)(2,1)} %copy.59), calls=%async_computation | async-start | bytes 3932160 | tf_op jit(solution)/shard_map/all_to_all | solution.py:217
  394.5 243.8 %all-gather.7.cloned.1.call-start = ((), (), s32[]{:S(2)}) async-start(), calls=%async_computation.6 | async-start | bytes 2211840 | tf_op jit(solution)/shard_map/all_gather | solution.py:206
  457.3 131.3 %all-to-all-start.1 = ((bf16[10,480,128]{2,0,1:T(8,128)(2,1)}), bf16[10,480,128]{2,0,1:T(8,128)(2,1)}, u32[]{:S(2)}, u32[]{:S(2)}) async-start(bf16[10,480,128]{2,0,1:T(8,128)(2,1)} %copy.66), calls=%async_computation.1 | async-start | bytes 3932160 | tf_op jit(solution)/shard_map/all_to_all | solution.py:216
  527.4 2.5 copy-start.18
  638.3 2.5 copy-start.14
  638.3 2.5 copy-start.15
  640.6 1.5 copy-start.8
  640.6 2.0 copy-start.9
  642.5 4.4 copy-start.10
  642.5 4.4 copy-start.12
  658.6 16.2 %copy-start.19 = (f32[32]{0:T(128)S(1)}, f32[32]{0:T(128)}, u32[]{:S(2)}) copy-start(f32[32]{0:T(128)} %param.17) | copy-start | bytes 388
  658.6 46.4 %all-to-all-start.2 = ((bf16[320,15,128]{2,1,0:T(8,128)(2,1)}), bf16[320,15,128]{2,1,0:T(8,128)(2,1)}, u32[]{:S(2)}, u32[]{:S(2)}) async-start(bf16[320,15,128]{2,1,0:T(8,128)(2,1)} %copy.72), calls=%async_computation.2 | async-start | bytes 2621440 | tf_op jit(solution)/shard_map/all_to_all | solution.py:223
  713.6 1.5 copy-start.6
  715.1 2.9 copy-start.3
  716.9 1.2 copy-start.4
  749.2 68.8 %all-to-all-start.3 = ((bf16[10,480,128]{2,0,1:T(8,128)(2,1)}), bf16[10,480,128]{2,0,1:T(8,128)(2,1)}, u32[]{:S(2)}, u32[]{:S(2)}) async-start(bf16[10,480,128]{2,0,1:T(8,128)(2,1)} %copy.77), calls=%async_computation.3 | async-start | bytes 3932160 | tf_op jit(solution)/shard_map/all_to_all | solution.py:217
  757.3 132.6 %all-gather.9.cloned.1.call-start = ((), (), s32[]{:S(2)}) async-start(), calls=%async_computation.7 | async-start | bytes 2211840 | tf_op jit(solution)/shard_map/all_gather | solution.py:206
  818.1 125.1 %all-to-all-start.4 = ((bf16[10,480,128]{2,0,1:T(8,128)(2,1)}), bf16[10,480,128]{2,0,1:T(8,128)(2,1)}, u32[]{:S(2)}, u32[]{:S(2)}) async-start(bf16[10,480,128]{2,0,1:T(8,128)(2,1)} %copy.84), calls=%async_computation.4 | async-start | bytes 3932160 | tf_op jit(solution)/shard_map/all_to_all | solution.py:216
  987.5 6.1 copy-start.11
  987.5 6.1 copy-start.13
  1063.0 1.5 copy-start.7
  1064.5 2.6 copy-start.1
Sparse Core Ops, SparseCore 0:
  397.5 63.9 all-gather.6
  759.9 61.9 all-gather.8
where the time goes:
time: 1090 us; the launch traced here: 1070 us
  local copies, waits for them, and re-layouts  509 us (47%)
  blocking collectives  177 us (16%)
  waiting for transfers between devices  140 us (13%)
  other arithmetic  139 us (13%)
  starting transfers between devices  47.3 us (4%)
  matrix products  45.9 us (4%)
  between operations  14.4 us (1%)
    dynamic_update_slice x32, local copies, waits for them, and re-layouts, legendre_local(): lax.scan(unfold, (head_all, tail_all), jnp.arange(16, dtype=jnp.int32))  229 us
    all_gather x2, blocking collectives, shards(): lax.all_gather(traj_wind[step_idx], 'pert', axis=0, tiled=True)  127 us
    reshape x4, local copies, waits for them, and re-layouts, synthesis(): part_pairs = fourier.reshape(fourier.shape[0], fourier.shape[1], -1, 2)  125 us
    all_to_all x2, waiting for transfers between devices, shards(): lax.all_to_all(slope_rows, 'space', split_axis=1, concat_axis=0, tiled=True)  113 us
    all_to_all x1, blocking collectives, shards(): lax.all_to_all(wave_lat, 'space', split_axis=0, concat_axis=1, tiled=True)  50.1 us
    all_to_all x1, waiting for transfers between devices, shards(): lax.all_to_all(wave_lat, 'space', split_axis=0, concat_axis=1, tiled=True)  27.5 us
    all_to_all x2, local copies, waits for them, and re-layouts, shards(): lax.all_to_all(slope_rows, 'space', split_axis=1, concat_axis=0, tiled=True)  26.2 us
    all_to_all x2, local copies, waits for them, and re-layouts, shards(): lax.all_to_all(fourier_rows, 'space', split_axis=1, concat_axis=0, tiled=...  26 us
  transfers between devices with their start and end apart: 7, of which 3 were waited for; matrix products, arithmetic and copies ran while one was open for 17% of the time, Pallas kernels for 0%

commit v1 on v0

v1 whole, which is shorter than its diff:
```python
import math

import jax
import jax.numpy as jnp
import numpy as np
from jax import lax
from jax.experimental import pallas as pl
from jax.experimental.pallas import tpu as pltpu
from jax.sharding import PartitionSpec as P

NLAT = 480
NLON = 960
M = 320
VARS = 2
LEV = 32
STEPS = 2
SPACE = 32
SLOTS = M // SPACE
LATS = NLAT // SPACE
PAD = 16
HALF = (SPACE // 2) * PAD
COLS = 128
ROWS = COLS // 2
HK = M // 2
CHUNKS = 8
GROUP = 4
F32 = jnp.float32
BF16 = jnp.bfloat16
MESH = pl.DeviceIdType.MESH
HIGHEST = lax.Precision.HIGHEST


def dot(a, b, dims=((1,), (0,)), precision=None):
    return lax.dot_general(
        a, b, (dims, ((), ())), preferred_element_type=F32, precision=precision
    )


def iota(shape, axis):
    return lax.broadcasted_iota(jnp.int32, shape, axis)


def reordered(old, new):
    part, row = new // ROWS, new % ROWS
    level = row // 8 * 4 + row % 4
    variable = row % 8 // 4
    return old == variable * 64 + level * 2 + part


def northern():
    place = np.arange(HALF)
    inside = place % PAD < LATS
    lat = np.minimum(place // PAD * LATS + place % PAD, NLAT // 2 - 1)
    angle = (lat + 0.5) * (math.pi / NLAT)
    weight = np.where(inside, np.sin(angle) * (math.pi / NLAT), 0.0)
    rows = np.stack([np.cos(angle), np.log(np.sin(angle)), inside.astype(np.float64)])
    return rows.astype(np.float32), np.repeat(weight[:, None], COLS, 1).astype(np.float32)


def table_kernel(
    wave_smem, wave_ref, lat_ref, spectra_ref, modes_ref, speeds_ref,
    table_ref, state_ref, send_ref, mix_ref, speed_ref, scratch,
):
    lev = iota((LEV, COLS), 0)
    column = iota((LEV, COLS), 1)
    onehot = (column // 2 % LEV == lev).astype(F32)
    spread = dot(onehot, modes_ref[...], ((0,), (1,)), HIGHEST)
    group = lambda c: c // (2 * LEV) * 2 + c % 2
    same = group(iota((COLS, COLS), 0)) == group(iota((COLS, COLS), 1))
    mix_ref[...] = dot(spread, onehot, precision=HIGHEST) * same.astype(F32)
    speed_ref[...] = dot(speeds_ref[...], onehot, precision=HIGHEST)

    wave = wave_ref[...]
    cosines = [lat_ref[0:1, c * 128 : (c + 1) * 128] for c in range(2)]
    number = (iota((16, 384), 1) + 1).astype(F32)
    terms = jnp.where(number <= wave[:, 0:1], jnp.log((2.0 * number + 1.0) / (2.0 * number)), 0.0)
    start = 0.5 * jnp.sum(terms, axis=1, keepdims=True) - 0.5 * math.log(2.0)
    starts = [
        start + wave * lat_ref[1:2, c * 128 : (c + 1) * 128] for c in range(2)
    ]
    inside = [lat_ref[2:3, c * 128 : (c + 1) * 128] for c in range(2)]

    def block(b, carry):
        current, previous, logs, last = carry
        current, previous, logs = list(current), list(previous), list(logs)
        factor = [jnp.exp(starts[c] + logs[c]) * inside[c] for c in range(2)]
        first = b * 16
        for i in range(16):
            k = (first + i).astype(F32)
            keep = (wave + k <= M - 1.0).astype(F32)
            row = (i % 2) * HK + b * 8 + i // 2
            for c in range(2):
                scratch[c, pl.ds(row, 16, stride=M), :] = current[c] * (factor[c] * keep)
            up = k + 1.0
            degree2 = 2.0 * (wave + up)
            coef = jnp.sqrt((degree2 * degree2 - 1.0) / (up * (2.0 * wave + up)))
            ratio = coef / last
            for c in range(2):
                following = coef * cosines[c] * current[c] - ratio * previous[c]
                previous[c] = current[c]
                current[c] = following
            last = coef
        for c in range(2):
            biggest = jnp.maximum(jnp.abs(current[c]), jnp.abs(previous[c]))
            shrink = 1.0 / biggest
            current[c] = current[c] * shrink
            previous[c] = previous[c] * shrink
            logs[c] = logs[c] + jnp.log(biggest)
        return tuple(current), tuple(previous), tuple(logs), last

    ones = jnp.ones((16, 128), F32)
    zeros = jnp.zeros((16, 128), F32)
    lax.fori_loop(0, M // 16, block, ((ones, ones), (zeros, zeros), (zeros, zeros), ones))

    perm = reordered(iota((COLS, COLS), 0), iota((COLS, COLS), 1)).astype(BF16)
    imaginary = iota((HK, COLS), 1) % 2 == 1
    half_degree = 2 * iota((HK, COLS), 0)

    def slot(j, _):
        w = wave_smem[j]
        for parity in range(2):
            for c in range(2):
                table_ref[j, parity, :, c * 128 : (c + 1) * 128] = scratch[
                    c, pl.ds(j * M + parity * HK, HK), :
                ].astype(BF16)
            keep = (half_degree + (parity + w) <= M - 1) & jnp.logical_not(imaginary & (w == 0))
            state_ref[j, parity] = spectra_ref[j, pl.ds(parity, HK, stride=2), :] * keep.astype(F32)
        legendre_rows(j, table_ref, state_ref[j, 0], state_ref[j, 1], perm, send_ref)
        return 0

    lax.fori_loop(0, SLOTS, slot, 0)


def legendre_rows(j, table_ref, even_state, odd_state, perm, send_ref):
    even = dot(
        table_ref[j, 0], dot(even_state.astype(BF16), perm).astype(BF16), ((0,), (0,))
    )
    odd = dot(
        table_ref[j, 1], dot(odd_state.astype(BF16), perm).astype(BF16), ((0,), (0,))
    )
    north = (even + odd).astype(BF16)
    south = (even - odd).astype(BF16)
    for d in range(SPACE // 2):
        send_ref[d, j] = north[d * PAD : (d + 1) * PAD]
        send_ref[SPACE - 1 - d, j] = south[d * PAD : (d + 1) * PAD]


def update_kernel(last, wave_smem, weight_ref, table_ref, state_ref, rows_ref, mix_ref, speed_ref, *outs):
    perm = reordered(iota((COLS, COLS), 1), iota((COLS, COLS), 0)).astype(BF16)
    perm_forward = reordered(iota((COLS, COLS), 0), iota((COLS, COLS), 1)).astype(BF16)
    imaginary = iota((HK, COLS), 1) % 2 == 1
    half_degree = 2 * iota((HK, COLS), 0)
    weight = weight_ref[...]
    speed = speed_ref[0:1, :]

    def slot(j, _):
        w = wave_smem[j]
        north = jnp.concatenate([rows_ref[d, j] for d in range(SPACE // 2)], axis=0).astype(F32)
        south = jnp.concatenate(
            [rows_ref[SPACE - 1 - d, j] for d in range(SPACE // 2)], axis=0
        ).astype(F32)
        new = []
        for parity in range(2):
            both = (north + south if parity == 0 else north - south) * weight
            columns = dot(both.astype(BF16), perm).astype(BF16)
            change = dot(table_ref[j, parity], columns)
            combined = state_ref[j, parity] + change
            degree = half_degree + (parity + w)
            keep = (degree <= M - 1) & jnp.logical_not(imaginary & (w == 0))
            stiffness = speed * (degree * (degree + 1)).astype(F32)
            damping = stiffness / (1.0 + stiffness)
            projected = dot(combined, mix_ref[...], precision=HIGHEST)
            returned = dot(damping * projected, mix_ref[...], ((1,), (1,)), HIGHEST)
            new.append((combined - returned) * keep.astype(F32))
        if last:
            for parity in range(2):
                outs[0][j, pl.ds(parity, HK, stride=2), :] = new[parity]
        else:
            for parity in range(2):
                outs[0][j, parity] = new[parity]
            legendre_rows(j, table_ref, new[0], new[1], perm_forward, outs[1])
        return 0

    lax.fori_loop(0, SLOTS, slot, 0)


def zonal_kernel(wave_ref, synth_ref, analysis_ref):
    wave = wave_ref[...]
    step = 2.0 * math.pi / NLON

    def angle_of(count):
        return (count - NLON * jnp.floor(count * (1.0 / NLON))) * step

    x = iota((M, 128), 1).astype(F32)
    angle = angle_of(wave * x)
    turn = angle_of(wave * jnp.full((M, 128), 128.0, F32))
    cosine, sine = jnp.cos(angle), jnp.sin(angle)
    turn_cosine, turn_sine = jnp.cos(turn), jnp.sin(turn)
    factor = jnp.where(wave == 0.0, 1.0, 2.0)
    for c in range(CHUNKS):
        width = min(128, NLON - c * 128)
        lanes = slice(c * 128, c * 128 + width)
        synth_ref[0:M, lanes] = (factor * cosine)[:, :width].astype(BF16)
        synth_ref[M : 2 * M, lanes] = (-factor * sine)[:, :width].astype(BF16)
        analysis_ref[0:M, lanes] = (cosine * (1.0 / NLON))[:, :width].astype(BF16)
        analysis_ref[M : 2 * M, lanes] = (sine * (-1.0 / NLON))[:, :width].astype(BF16)
        cosine, sine = (
            cosine * turn_cosine - sine * turn_sine,
            sine * turn_cosine + cosine * turn_sine,
        )


def grid_kernel(flip_smem, wave_ref, rows_ref, synth_ref, analysis_ref, traj_ref, out_ref, wide, narrow):
    g = pl.program_id(0)

    @pl.when(g == 0)
    def _():
        def widen(i, _):
            at = pl.ds(pl.multiple_of(i * 512, 512), 512)
            wide[at, :] = rows_ref[at, :].astype(F32)
            return 0

        lax.fori_loop(0, M * PAD // 512, widen, 0)

    wave = wave_ref[...]
    low = iota((M, COLS), 1) < ROWS
    values_in, slopes_in = [], []
    for pair in range(GROUP // 2):
        t = g * GROUP + 2 * pair
        one = wide[pl.ds(t, M, stride=PAD), :]
        two = wide[pl.ds(t + 1, M, stride=PAD), :]
        real = jnp.where(low, one, pltpu.roll(two, ROWS, 1))
        imag = jnp.where(low, pltpu.roll(one, ROWS, 1), two)
        values_in.append(jnp.concatenate([real, imag], axis=0).astype(BF16))
        slopes_in.append(jnp.concatenate([-wave * imag, wave * real], axis=0).astype(BF16))
    values = dot(jnp.concatenate(values_in, axis=1), synth_ref[...], ((0,), (0,)))
    slopes = dot(jnp.concatenate(slopes_in, axis=1), synth_ref[...], ((0,), (0,)))
    pieces = []
    for q in range(GROUP):
        i = jnp.minimum(g * GROUP + q, LATS - 1)
        t = jnp.where(flip_smem[0] == 1, LATS - 1 - i, i)
        now = traj_ref[:, t].astype(F32)
        wind = jnp.concatenate([now[:, 0], now[:, 0]], axis=1)
        state = jnp.concatenate([now[:, 2], now[:, 1]], axis=1)
        v = values[q * ROWS : (q + 1) * ROWS].reshape(8, 8, NLON)
        s = slopes[q * ROWS : (q + 1) * ROWS].reshape(8, 8, NLON)
        pieces.append((-wind * s - state * v).reshape(ROWS, NLON).astype(BF16))
    forcing = jnp.concatenate(pieces, axis=0)
    waves = dot(analysis_ref[...], forcing, ((1,), (1,)))
    for pair in range(GROUP // 2):
        t = g * GROUP + 2 * pair
        real = waves[0:M, pair * COLS : (pair + 1) * COLS]
        imag = waves[M : 2 * M, pair * COLS : (pair + 1) * COLS]
        narrow[pl.ds(t, M, stride=PAD), :] = jnp.where(low, real, pltpu.roll(imag, ROWS, 1))
        narrow[pl.ds(t + 1, M, stride=PAD), :] = jnp.where(low, pltpu.roll(real, ROWS, 1), imag)

    @pl.when(g == PAD // GROUP - 1)
    def _():
        def shrink(i, _):
            at = pl.ds(pl.multiple_of(i * 512, 512), 512)
            out_ref[at, :] = narrow[at, :].astype(BF16)
            return 0

        lax.fori_loop(0, M * PAD // 512, shrink, 0)


def exchange_kernel(src, dst, send_sem, recv_sem, own_sem):
    me = lax.axis_index("space")
    barrier = pltpu.get_barrier_semaphore()

    def greet(i, _):
        pl.semaphore_signal(
            barrier, inc=1, device_id={"space": lax.rem(me + i, SPACE)}, device_id_type=MESH
        )
        return 0

    lax.fori_loop(1, SPACE, greet, 0)
    pl.semaphore_wait(barrier, SPACE - 1)
    own = pltpu.make_async_copy(src.at[me], dst.at[me], own_sem)
    own.start()

    def copy(i):
        to = lax.rem(me + i, SPACE)
        return pltpu.make_async_remote_copy(
            src.at[to], dst.at[me], send_sem.at[i], recv_sem.at[i],
            device_id={"space": to}, device_id_type=MESH,
        )

    def start(i, _):
        copy(i).start()
        return 0

    lax.fori_loop(1, SPACE, start, 0)
    own.wait()

    def finish(i, _):
        origin = lax.rem(me - i + SPACE, SPACE)
        pltpu.make_async_remote_copy(
            src.at[origin], dst.at[origin], send_sem.at[i], recv_sem.at[i],
            device_id={"space": origin}, device_id_type=MESH,
        ).wait_recv()
        copy(i).wait_send()
        return 0

    lax.fori_loop(1, SPACE, finish, 0)


VMEM = pl.BlockSpec(memory_space=pltpu.VMEM)
SMEM = pl.BlockSpec(memory_space=pltpu.SMEM)
PARAMS = pltpu.CompilerParams(vmem_limit_bytes=56 * 2**20)


def exchange(x):
    return pl.pallas_call(
        exchange_kernel,
        out_shape=jax.ShapeDtypeStruct(x.shape, x.dtype),
        in_specs=[pl.BlockSpec(memory_space=pl.ANY)],
        out_specs=pl.BlockSpec(memory_space=pl.ANY),
        scratch_shapes=[
            pltpu.SemaphoreType.DMA((SPACE,)),
            pltpu.SemaphoreType.DMA((SPACE,)),
            pltpu.SemaphoreType.DMA,
        ],
        compiler_params=pltpu.CompilerParams(collective_id=1, has_side_effects=True),
        name="exchange",
    )(x)


def grid_stage(flip, wave_rows, rows, synth, analysis, traj):
    whole = lambda shape: pl.BlockSpec(shape, lambda g: (0,) * len(shape), pipeline_mode=pl.Buffered(1))
    return pl.pallas_call(
        grid_kernel,
        grid=(PAD // GROUP,),
        out_shape=jax.ShapeDtypeStruct((M * PAD, COLS), BF16),
        in_specs=[
            SMEM,
            whole((M, 1)),
            whole((M * PAD, COLS)),
            whole((2 * M, NLON)),
            whole((2 * M, NLON)),
            whole((8, LATS, 3, 4, NLON)),
        ],
        out_specs=pl.BlockSpec((M * PAD, COLS), lambda g: (0, 0), pipeline_mode=pl.Buffered(1)),
        scratch_shapes=[pltpu.VMEM((M * PAD, COLS), F32), pltpu.VMEM((M * PAD, COLS), F32)],
        compiler_params=PARAMS,
        name="grid_stage",
    )(flip, wave_rows, rows, synth, analysis, traj)


def shards(spectra, wave_order, traj_wind, traj_state, vertical_modes, mode_speeds):
    space = lax.axis_index("space")
    lat_rows, weight = northern()
    gathered = []
    for step in range(STEPS):
        fields = jnp.concatenate([traj_wind[step][None], traj_state[step]], axis=0)
        fields = jnp.transpose(fields, (2, 0, 1, 3))
        gathered.append(lax.all_gather(fields, "pert", axis=0))
    wave_here = lax.dynamic_slice_in_dim(wave_order, space * SLOTS, SLOTS)
    wave_wide = jnp.broadcast_to(
        jnp.pad(wave_here, (0, 16 - SLOTS)).astype(F32)[:, None], (16, 128)
    )
    wave_rows = wave_order.astype(F32)[:, None]
    flip = (space >= SPACE // 2).astype(jnp.int32)[None]
    speeds = jnp.broadcast_to(mode_speeds[None], (8, LEV))

    send_shape = jax.ShapeDtypeStruct((SPACE, SLOTS, PAD, COLS), BF16)
    state_shape = jax.ShapeDtypeStruct((SLOTS, 2, HK, COLS), F32)
    table, state, send, mix, speed = pl.pallas_call(
        table_kernel,
        out_shape=(
            jax.ShapeDtypeStruct((SLOTS, 2, HK, HALF), BF16),
            state_shape,
            send_shape,
            jax.ShapeDtypeStruct((COLS, COLS), F32),
            jax.ShapeDtypeStruct((8, COLS), F32),
        ),
        in_specs=[SMEM] + [VMEM] * 5,
        out_specs=(VMEM,) * 5,
        scratch_shapes=[pltpu.VMEM((2, 16 * M, 128), F32)],
        compiler_params=PARAMS,
        name="table_stage",
    )(wave_here, wave_wide, jnp.asarray(lat_rows), spectra, vertical_modes, speeds)
    synth, analysis = pl.pallas_call(
        zonal_kernel,
        out_shape=(jax.ShapeDtypeStruct((2 * M, NLON), BF16),) * 2,
        in_specs=[VMEM],
        out_specs=(VMEM,) * 2,
        compiler_params=PARAMS,
        name="zonal_stage",
    )(wave_rows)

    for step in range(STEPS):
        rows = exchange(send).reshape(M * PAD, COLS)
        waves = grid_stage(flip, wave_rows, rows, synth, analysis, gathered[step])
        back = exchange(waves.reshape(SPACE, SLOTS, PAD, COLS))
        last = step == STEPS - 1
        result = pl.pallas_call(
            lambda *refs, last=last: update_kernel(last, *refs),
            out_shape=jax.ShapeDtypeStruct((SLOTS, M, COLS), F32) if last else (state_shape, send_shape),
            in_specs=[SMEM] + [VMEM] * 6,
            out_specs=VMEM if last else (VMEM, VMEM),
            compiler_params=PARAMS,
            name="last_update" if last else "update",
        )(wave_here, jnp.asarray(weight), table, state, back, mix, speed)
        if last:
            return result
        state, send = result


def solution(mesh):
    placed = (
        P("space", None, "pert"),
        P(),
        P(None, "pert", "space", None),
        P(None, None, "pert", "space", None),
        P(),
        P(),
    )
    return jax.shard_map(
        shards, mesh=mesh, in_specs=placed, out_specs=P("space", None, "pert"), check_vma=False
    )
```

time: 1090 us -> 292 us (0.27); the launches traced: 1070 us -> 292 us
  local copies, waits for them, and re-layouts: 509 us -> 13.4 us
  Pallas kernels: 0 us -> 263 us
  blocking collectives: 177 us -> 0 us
  waiting for transfers between devices: 140 us -> 0.06 us
  other arithmetic: 139 us -> 1.99 us
  starting transfers between devices: 47.3 us -> 0.04 us
  matrix products: 45.9 us -> 0 us
    pallas_call x0 -> x10, Pallas kernels: none -> 263 us  [the longest x4 181 us: exchange(): pl.pallas_call(exchange_kernel, out_shape=jax.ShapeDtypeStruct(x.shape, x...]
    dynamic_update_slice x32 -> x0, local copies, waits for them, and re-layouts: 229 us -> none  [legendre_local(): lax.scan(unfold, (head_all, tail_all), jnp.arange(16, dtype=jnp.int32))]
    all_to_all x5 -> x0, waiting for transfers between devices: 140 us -> none  [the longest x2 113 us: shards(): lax.all_to_all(slope_rows, 'space', split_axis=1, concat_axis=0, tiled=True)]
    reshape x8 -> x0, local copies, waits for them, and re-layouts: 140 us -> none  [the longest x4 125 us: synthesis(): part_pairs = fourier.reshape(fourier.shape[0], fourier.shape[1], -1, 2)]
    all_gather x2 -> x0, blocking collectives: 127 us -> none  [shards(): lax.all_gather(traj_wind[step_idx], 'pert', axis=0, tiled=True)]
    all_to_all x8 -> x0, local copies, waits for them, and re-layouts: 62.5 us -> none  [the longest x2 26.2 us: shards(): lax.all_to_all(slope_rows, 'space', split_axis=1, concat_axis=0, tiled=True)]
    all_to_all x1 -> x0, blocking collectives: 50.1 us -> none  [shards(): lax.all_to_all(wave_lat, 'space', split_axis=0, concat_axis=1, tiled=True)]
    all_to_all x5 -> x0, starting transfers between devices: 47.2 us -> none  [the longest x2 20.6 us: shards(): lax.all_to_all(slope_rows, 'space', split_axis=1, concat_axis=0, tiled=True)]
  transfers between devices with their start and end apart: 7 -> 2, of which waited for: 3 -> 0; matrix products, arithmetic and copies ran while one was open for 17% -> 3% of each run, Pallas kernels for 0% -> 67%
where the time goes in v1:
time: 292 us
  Pallas kernels  263 us (90%)
  between operations  13.5 us (5%)
  local copies, waits for them, and re-layouts  13.4 us (5%)
    pallas_call x4, Pallas kernels, exchange(): pl.pallas_call(exchange_kernel, out_shape=jax.ShapeDtypeStruct(x.shape, x...  181 us
    pallas_call x2, Pallas kernels, shards(): pl.pallas_call(lambda *refs, last=last: update_kernel(last, *refs), out_s...  36 us
    pallas_call x2, Pallas kernels, grid_stage(): pl.pallas_call(grid_kernel, grid=(PAD // GROUP,), out_shape=jax.ShapeDtyp...  26.6 us
    pallas_call x1, Pallas kernels, shards(): pl.pallas_call(table_kernel, out_shape=(jax.ShapeDtypeStruct((SLOTS, 2, H...  14.5 us
    all_gather x2, local copies, waits for them, and re-layouts, shards(): gathered.append(lax.all_gather(fields, 'pert', axis=0))  8.98 us
  transfers between devices with their start and end apart: 2, of which 0 were waited for; matrix products, arithmetic and copies ran while one was open for 3% of the time, Pallas kernels for 67%

profile of v1, /device:TPU:1, one launch (start us, length us, event | category | flops | bytes accessed | tf_op | source)
XLA Modules:
  0.0 291.6 jit_solution(5972907169705855871)
XLA Ops:
  6.5 0.0 all-gather.5.cloned.1.call-start
  6.5 1.2 slice_bitcast_fusion
  7.8 0.0 copy-start.1
  7.8 0.0 copy-start.2
  7.8 1.1 fusion
  8.9 1.0 maximum_bitcast_fusion
  9.9 0.0 all-gather.5.cloned.1.call-update
  9.9 0.0 all-gather.7.cloned.1.call-start
  9.9 1.0 maximum_bitcast_fusion.1
  10.9 0.0 all-gather.7.cloned.1.call-update
  11.0 0.0 copy-done.1
  11.0 0.1 dynamic_slice.3.wave_smem.refs_0_
  11.1 0.0 copy-start
  11.1 0.7 broadcast_in_dim.20.wave_ref
  11.7 0.0 copy-done.2
  11.7 0.6 broadcast_in_dim.21.speeds_ref
  12.3 0.0 copy-done
  12.3 14.5 %table_stage.1 = (bf16[10,2,160,256]{3,2,1,0:T(8,128)(2,1)}, f32[10,2,160,128]{3,2,1,0:T(8,128)}, bf16[32,10,16,128]{3,2,1,0:T(8,128)(2,1)}, f32[128,128]{1,0:T(8,128)}, f32[8,128]{1,0:T(8,128)}) custom-call(s32[10]{0:T(128)} %copy-done, f32[16,128]{1,0:T(8,128)} %broadcast_in_dim.20.wave_ref, f32[3,256]{1,0:T(4,128)} %constant.16.clone.lat_ref, ...), custom_call_target="tpu_custom_call" | custom-call | tf_op jit(solution)/shard_map/table_stage/pallas_call | solution.py:368
  26.8 54.9 %exchange.4 = bf16[32,10,16,128]{3,2,1,0:T(8,128)(2,1)} custom-call(bf16[32,10,16,128]{3,2,1,0:T(8,128)(2,1)} %get-tuple-element.16.src), custom_call_target="tpu_custom_call" | custom-call | tf_op jit(solution)/shard_map/exchange/pallas_call | solution.py:314
  81.7 0.8 broadcast_in_dim.26.wave_ref
  82.5 4.6 %zonal_stage.1 = (bf16[640,960]{1,0:T(8,128)(2,1)}, bf16[640,960]{1,0:T(8,128)(2,1)}) custom-call(f32[320,1]{1,0:T(8,128)} %broadcast_in_dim.26.wave_ref), custom_call_target="tpu_custom_call" | custom-call | tf_op jit(solution)/shard_map/zonal_stage/pallas_call | solution.py:383
  87.2 0.0 all-gather.5.cloned.1.call-done
  87.2 4.5 %copy.12 = bf16[120,3,4,960]{3,2,1,0:T(4,128)(2,1)} copy(bf16[120,3,4,960]{3,2,0,1:T(4,128)(2,1)} %all-gather.5.cloned.1.call-done) | data formatting | bytes 5529600 | tf_op jit(solution)/shard_map/all_gather | solution.py:357
  91.7 13.3 %grid_stage.2 = bf16[5120,128]{1,0:T(8,128)(2,1)} custom-call(s32[1]{0:T(128)} %bitcast.flip_smem, f32[320,1]{1,0:T(8,128)} %broadcast_in_dim.26.wave_ref, bf16[5120,128]{1,0:T(8,128)(2,1)} %bitcast.17, bf16[640,960]{1,0:T(8,128)(2,1)} %get-tuple-element.17.synth_ref, bf16[640,960]{1,0:T(8,128)(2,1)} %get-tuple-element.18.analysis_ref, ...), custom_call_target="tpu_custom_call" | custom-call | tf_op jit(solution)/shard_map/grid_stage/pallas_call | solution.py:331
  105.0 51.6 %exchange.5.refs_4_ = bf16[32,10,16,128]{3,2,1,0:T(8,128)(2,1)} custom-call(bf16[32,10,16,128]{3,2,1,0:T(8,128)(2,1)} %bitcast.20), custom_call_target="tpu_custom_call" | custom-call | tf_op jit(solution)/shard_map/exchange/pallas_call | solution.py:314
  156.6 19.6 %update.1 = (f32[10,2,160,128]{3,2,1,0:T(8,128)}, bf16[32,10,16,128]{3,2,1,0:T(8,128)(2,1)}) custom-call(s32[10]{0:T(128)} %copy-done, f32[256,128]{1,0:T(8,128)} %constant.17.clone.refs_1_, bf16[10,2,160,256]{3,2,1,0:T(8,128)(2,1)} %get-tuple-element.14.refs_2_, f32[10,2,160,128]{3,2,1,0:T(8,128)} %get-tuple-element.15.refs_3_, ...), custom_call_target="tpu_custom_call" | custom-call | tf_op jit(solution)/shard_map/update/pallas_call | solution.py:397
  176.2 37.7 %exchange.6 = bf16[32,10,16,128]{3,2,1,0:T(8,128)(2,1)} custom-call(bf16[32,10,16,128]{3,2,1,0:T(8,128)(2,1)} %get-tuple-element.22.src), custom_call_target="tpu_custom_call" | custom-call | tf_op jit(solution)/shard_map/exchange/pallas_call | solution.py:314
  213.9 0.0 all-gather.7.cloned.1.call-done
  214.0 4.5 %copy.14 = bf16[120,3,4,960]{3,2,1,0:T(4,128)(2,1)} copy(bf16[120,3,4,960]{3,2,0,1:T(4,128)(2,1)} %all-gather.7.cloned.1.call-done) | data formatting | bytes 5529600 | tf_op jit(solution)/shard_map/all_gather | solution.py:357
  218.4 13.3 %grid_stage.3 = bf16[5120,128]{1,0:T(8,128)(2,1)} custom-call(s32[1]{0:T(128)} %bitcast.flip_smem, f32[320,1]{1,0:T(8,128)} %broadcast_in_dim.26.wave_ref, bf16[5120,128]{1,0:T(8,128)(2,1)} %bitcast.18, bf16[640,960]{1,0:T(8,128)(2,1)} %get-tuple-element.17.synth_ref, bf16[640,960]{1,0:T(8,128)(2,1)} %get-tuple-element.18.analysis_ref, ...), custom_call_target="tpu_custom_call" | custom-call | tf_op jit(solution)/shard_map/grid_stage/pallas_call | solution.py:331
  231.7 36.7 %exchange.7.refs_4_ = bf16[32,10,16,128]{3,2,1,0:T(8,128)(2,1)} custom-call(bf16[32,10,16,128]{3,2,1,0:T(8,128)(2,1)} %bitcast.19), custom_call_target="tpu_custom_call" | custom-call | tf_op jit(solution)/shard_map/exchange/pallas_call | solution.py:314
  268.4 16.4 %last_update.1 = f32[10,320,128]{2,1,0:T(8,128)} custom-call(s32[10]{0:T(128)} %copy-done, f32[256,128]{1,0:T(8,128)} %constant.17.clone.refs_1_, bf16[10,2,160,256]{3,2,1,0:T(8,128)(2,1)} %get-tuple-element.14.refs_2_, f32[10,2,160,128]{3,2,1,0:T(8,128)} %get-tuple-element.21.refs_3_, bf16[32,10,16,128]{3,2,1,0:T(8,128)(2,1)} %exchange.7.refs_4_, ...), custom_call_target="tpu_custom_call" | custom-call | tf_op jit(solution)/shard_map/last_update/pallas_call | solution.py:397
  (2 shorter events, 0.0 us)
Async XLA Ops:
  6.5 80.6 %all-gather.5.cloned.1.call-start = ((), (), s32[]{:S(2)}) async-start(), calls=%async_computation | async-start | bytes 3317760 | tf_op jit(solution)/shard_map/all_gather | solution.py:357
  7.8 3.2 %copy-start.1 = (s32[320]{0:T(512)S(1)}, s32[320]{0:T(512)}, u32[]{:S(2)}) copy-start(s32[320]{0:T(512)} %param.9) | copy-start | bytes 3844
  7.8 3.9 %copy-start.2 = (f32[32]{0:T(128)S(1)}, f32[32]{0:T(128)}, u32[]{:S(2)}) copy-start(f32[32]{0:T(128)} %param.13) | copy-start | bytes 388
  9.9 204.1 %all-gather.7.cloned.1.call-start = ((), (), s32[]{:S(2)}) async-start(), calls=%async_computation.1 | async-start | bytes 3317760 | tf_op jit(solution)/shard_map/all_gather | solution.py:357
  11.1 1.3 copy-start
Sparse Core Ops, SparseCore 0:
  10.0 74.6 all-gather.4
  86.5 72.0 all-gather.6

commit v2 on v1

v2 whole, which is shorter than its diff:
```python
import math

import jax
import jax.numpy as jnp
import numpy as np
from jax import lax
from jax.experimental import pallas as pl
from jax.experimental.pallas import tpu as pltpu
from jax.sharding import PartitionSpec as P

NLAT = 480
NLON = 960
M = 320
VARS = 2
LEV = 32
STEPS = 2
PERT = 8
SPACE = 32
SLOTS = M // SPACE
LATS = NLAT // SPACE
PAD = 16
HALF = (SPACE // 2) * PAD
COLS = 128
ROWS = COLS // 2
HK = M // 2
CHUNKS = 8
GROUP = 4
F32 = jnp.float32
BF16 = jnp.bfloat16
MESH = pl.DeviceIdType.MESH
HIGHEST = lax.Precision.HIGHEST


def dot(a, b, dims=((1,), (0,)), precision=None):
    return lax.dot_general(
        a, b, (dims, ((), ())), preferred_element_type=F32, precision=precision
    )


def iota(shape, axis):
    return lax.broadcasted_iota(jnp.int32, shape, axis)


def level_of(new):
    return new % ROWS // 8 * 4 + new % 4


def group_of(new):
    return new // ROWS * 2 + new % 8 // 4


def reordered(old, new):
    return old == new % 8 // 4 * 64 + level_of(new) * 2 + new // ROWS


def split(x):
    high = x.astype(BF16)
    return jnp.concatenate([high, (x - high.astype(F32)).astype(BF16)], axis=1)


def northern():
    place = np.arange(HALF)
    inside = place % PAD < LATS
    lat = np.minimum(place // PAD * LATS + place % PAD, NLAT // 2 - 1)
    angle = (lat + 0.5) * (math.pi / NLAT)
    rows = np.stack([np.cos(angle), np.log(np.sin(angle)), inside.astype(np.float64)])
    weight = np.sin((np.arange(NLAT // 2) + 0.5) * (math.pi / NLAT)) * (math.pi / NLAT)
    return rows.astype(np.float32), weight.astype(np.float32)


def keep_of(w):
    row = iota((M, COLS), 0)
    degree = jnp.where(row < HK, 2 * row, 2 * row - (M - 1)) + w
    keep = (degree <= M - 1) & jnp.logical_not((iota((M, COLS), 1) >= ROWS) & (w == 0))
    return keep.astype(F32), degree


def legendre_rows(j, table_ref, state, send_ref):
    even, odd = state[:HK], state[HK:]
    both = jnp.concatenate(
        [jnp.concatenate([even, even], axis=1), jnp.concatenate([odd, -odd], axis=1)], axis=0
    )
    rows = dot(table_ref[j], both, ((0,), (0,))).astype(BF16)
    for d in range(SPACE // 2):
        send_ref[d, j] = rows[d * PAD : (d + 1) * PAD, :COLS]
        send_ref[SPACE - 1 - d, j] = rows[d * PAD : (d + 1) * PAD, COLS:]


def table_kernel(
    wave_smem, lat_ref, spectra_ref, modes_ref, speeds_ref,
    table_ref, state_ref, send_ref, mix_ref, speed_ref, scratch,
):
    lev = iota((LEV, COLS), 0)
    onehot = (level_of(iota((LEV, COLS), 1)) == lev).astype(F32)
    same = (group_of(iota((COLS, COLS), 0)) == group_of(iota((COLS, COLS), 1))).astype(F32)
    for way in range(2):
        spread = dot(onehot, modes_ref[...], ((0,), (1 - way,)), HIGHEST)
        mix = dot(spread, onehot, precision=HIGHEST) * same
        high = mix.astype(BF16)
        low = (mix - high.astype(F32)).astype(BF16)
        mix_ref[way, :COLS, :COLS] = high
        mix_ref[way, :COLS, COLS:] = low
        mix_ref[way, COLS:, :COLS] = high
        mix_ref[way, COLS:, COLS:] = jnp.zeros_like(low)
    speed_ref[...] = dot(jnp.broadcast_to(speeds_ref[...], (8, LEV)), onehot, precision=HIGHEST)

    base = lax.axis_index("space") * SLOTS
    row16 = iota((16, 128), 0)
    wave = jnp.zeros((16, 128), jnp.int32)
    for j in range(SLOTS):
        wave = jnp.where(row16 == j, wave_smem[base + j], wave)
    wave = wave.astype(F32)
    cosines = [lat_ref[0:1, c * 128 : (c + 1) * 128] for c in range(2)]
    number = (iota((16, 384), 1) + 1).astype(F32)
    terms = jnp.where(number <= wave[:, 0:1], jnp.log((2.0 * number + 1.0) / (2.0 * number)), 0.0)
    start = 0.5 * jnp.sum(terms, axis=1, keepdims=True) - 0.5 * math.log(2.0)
    starts = [start + wave * lat_ref[1:2, c * 128 : (c + 1) * 128] for c in range(2)]
    inside = [lat_ref[2:3, c * 128 : (c + 1) * 128] for c in range(2)]

    def block(b, carry):
        current, previous, logs, last = carry
        current, previous, logs = list(current), list(previous), list(logs)
        factor = [jnp.exp(starts[c] + logs[c]) * inside[c] for c in range(2)]
        first = b * 16
        for i in range(16):
            k = (first + i).astype(F32)
            keep = (wave + k <= M - 1.0).astype(F32)
            row = (i % 2) * HK + b * 8 + i // 2
            for c in range(2):
                scratch[c, pl.ds(row, 16, stride=M), :] = current[c] * (factor[c] * keep)
            up = k + 1.0
            degree2 = 2.0 * (wave + up)
            coef = jnp.sqrt((degree2 * degree2 - 1.0) / (up * (2.0 * wave + up)))
            ratio = coef / last
            for c in range(2):
                following = (coef * cosines[c]) * current[c] - ratio * previous[c]
                previous[c] = current[c]
                current[c] = following
            last = coef
        for c in range(2):
            biggest = jnp.maximum(jnp.abs(current[c]), jnp.abs(previous[c]))
            shrink = 1.0 / biggest
            current[c] = current[c] * shrink
            previous[c] = previous[c] * shrink
            logs[c] = logs[c] + jnp.log(biggest)
        return tuple(current), tuple(previous), tuple(logs), last

    ones = jnp.ones((16, 128), F32)
    zeros = jnp.zeros((16, 128), F32)
    lax.fori_loop(0, M // 16, block, ((ones, ones), (zeros, zeros), (zeros, zeros), ones))

    old, new = iota((2 * COLS, 2 * COLS), 0), iota((2 * COLS, 2 * COLS), 1)
    perm = (reordered(old % COLS, new % COLS) & (old // COLS == new // COLS)).astype(BF16)

    def slot(j, _):
        for c in range(2):
            table_ref[j, :, c * 128 : (c + 1) * 128] = scratch[c, pl.ds(j * M, M), :].astype(BF16)
        keep, _ = keep_of(wave_smem[base + j])
        given = jnp.concatenate(
            [spectra_ref[j, pl.ds(parity, HK, stride=2), :] for parity in range(2)], axis=0
        )
        moved = dot(split(given), perm)
        high = moved[:, :COLS] * keep
        state_ref[j] = high + moved[:, COLS:] * keep
        legendre_rows(j, table_ref, high.astype(BF16), send_ref)
        return 0

    lax.fori_loop(0, SLOTS, slot, 0)


def update_kernel(last, wave_smem, table_ref, state_ref, rows_ref, mix_ref, speed_ref, *outs):
    base = lax.axis_index("space") * SLOTS
    speed = speed_ref[0:1, :]
    new, old = iota((2 * COLS, COLS), 0), iota((2 * COLS, COLS), 1)
    perm = reordered(old, new % COLS).astype(BF16)

    def slot(j, _):
        rows = jnp.concatenate(
            [
                jnp.concatenate([rows_ref[d, j] for d in range(SPACE // 2)], axis=0),
                jnp.concatenate([rows_ref[SPACE - 1 - d, j] for d in range(SPACE // 2)], axis=0),
            ],
            axis=1,
        )
        change = dot(table_ref[j], rows)
        north, south = change[:, :COLS], change[:, COLS:]
        change = jnp.concatenate([north[:HK] + south[:HK], north[HK:] - south[HK:]], axis=0)
        combined = state_ref[j] + change
        keep, degree = keep_of(wave_smem[base + j])
        stiffness = speed * (degree * (degree + 1)).astype(F32)
        damping = stiffness / (1.0 + stiffness)
        projected = dot(split(combined), mix_ref[0])
        projected = damping * (projected[:, :COLS] + projected[:, COLS:])
        returned = dot(split(projected), mix_ref[1])
        result = (combined - (returned[:, :COLS] + returned[:, COLS:])) * keep
        if last:
            result = dot(split(result), perm)
            for parity in range(2):
                outs[0][j, pl.ds(parity, HK, stride=2), :] = result[parity * HK : (parity + 1) * HK]
        else:
            outs[0][j] = result
            legendre_rows(j, table_ref, result.astype(BF16), outs[1])
        return 0

    lax.fori_loop(0, SLOTS, slot, 0)


def zonal_tables(wave_ref, synth_ref, analysis_ref):
    step = 2.0 * math.pi / NLON

    def angle_of(count):
        return (count - NLON * jnp.floor(count * (1.0 / NLON))) * step

    def rows(i, _):
        at = pl.ds(pl.multiple_of(i * 64, 64), 64)
        below = pl.ds(pl.multiple_of(M + i * 64, 64), 64)
        wave = wave_ref[at, :]
        x = iota((64, 128), 1).astype(F32)
        angle = angle_of(wave * x)
        turn = angle_of(wave * jnp.full((64, 128), 128.0, F32))
        cosine, sine = jnp.cos(angle), jnp.sin(angle)
        turn_cosine, turn_sine = jnp.cos(turn), jnp.sin(turn)
        factor = jnp.where(wave == 0.0, 1.0, 2.0)
        for c in range(CHUNKS):
            width = min(128, NLON - c * 128)
            lanes = slice(c * 128, c * 128 + width)
            synth_ref[at, lanes] = (factor * cosine)[:, :width].astype(BF16)
            synth_ref[below, lanes] = (-factor * sine)[:, :width].astype(BF16)
            analysis_ref[at, lanes] = (cosine * (1.0 / NLON))[:, :width].astype(BF16)
            analysis_ref[below, lanes] = (sine * (-1.0 / NLON))[:, :width].astype(BF16)
            cosine, sine = (
                cosine * turn_cosine - sine * turn_sine,
                sine * turn_cosine + cosine * turn_sine,
            )
        return 0

    lax.fori_loop(0, M // 64, rows, 0)


def grid_kernel(weight_smem, wave_ref, rows_ref, synth_ref, analysis_ref, traj_ref, out_ref, wide, narrow):
    g = pl.program_id(0)
    space = lax.axis_index("space")
    flip = space >= SPACE // 2
    first_weight = jnp.where(flip, SPACE - 1 - space, space) * LATS

    @pl.when(g == 0)
    def _():
        def widen(i, _):
            at = pl.ds(pl.multiple_of(i * 512, 512), 512)
            wide[at, :] = rows_ref[at, :].astype(F32)
            return 0

        lax.fori_loop(0, M * PAD // 512, widen, 0)

    wave = wave_ref[...]
    low = iota((M, COLS), 1) < ROWS
    values_in, slopes_in = [], []
    for pair in range(GROUP // 2):
        t = g * GROUP + 2 * pair
        one = wide[pl.ds(t, M, stride=PAD), :]
        two = wide[pl.ds(t + 1, M, stride=PAD), :]
        real = jnp.where(low, one, pltpu.roll(two, ROWS, 1))
        imag = jnp.where(low, pltpu.roll(one, ROWS, 1), two)
        values_in.append(jnp.concatenate([real, imag], axis=0).astype(BF16))
        slopes_in.append(jnp.concatenate([-wave * imag, wave * real], axis=0).astype(BF16))
    values = dot(jnp.concatenate(values_in, axis=1), synth_ref[...], ((0,), (0,)))
    slopes = dot(jnp.concatenate(slopes_in, axis=1), synth_ref[...], ((0,), (0,)))
    pieces = []
    for q in range(GROUP):
        i = jnp.minimum(g * GROUP + q, LATS - 1)
        t = jnp.where(flip, LATS - 1 - i, i)
        now = traj_ref[:, t].astype(F32)
        wind = jnp.concatenate([now[:, 0], now[:, 0]], axis=1)
        state = jnp.concatenate([now[:, 2], now[:, 1]], axis=1)
        v = values[q * ROWS : (q + 1) * ROWS].reshape(8, 8, NLON)
        s = slopes[q * ROWS : (q + 1) * ROWS].reshape(8, 8, NLON)
        forcing = (wind * s + state * v) * -weight_smem[first_weight + i]
        pieces.append(forcing.reshape(ROWS, NLON).astype(BF16))
    forcing = jnp.concatenate(pieces, axis=0)
    waves = dot(analysis_ref[...], forcing, ((1,), (1,)))
    for pair in range(GROUP // 2):
        t = g * GROUP + 2 * pair
        real = waves[0:M, pair * COLS : (pair + 1) * COLS]
        imag = waves[M : 2 * M, pair * COLS : (pair + 1) * COLS]
        narrow[pl.ds(t, M, stride=PAD), :] = jnp.where(low, real, pltpu.roll(imag, ROWS, 1))
        narrow[pl.ds(t + 1, M, stride=PAD), :] = jnp.where(low, pltpu.roll(real, ROWS, 1), imag)

    @pl.when(g == PAD // GROUP - 1)
    def _():
        def shrink(i, _):
            at = pl.ds(pl.multiple_of(i * 512, 512), 512)
            out_ref[at, :] = narrow[at, :].astype(BF16)
            return 0

        lax.fori_loop(0, M * PAD // 512, shrink, 0)


def remote(src, dst, send, recv, **to):
    return pltpu.make_async_remote_copy(
        src, dst, send, recv, device_id=to, device_id_type=MESH
    )


def exchange_kernel(step, tables, *refs):
    refs = list(refs)
    src = refs.pop(0)
    if step is not None:
        own_ref, part_ref = refs.pop(0), refs.pop(0)
    if tables:
        wave_ref = refs.pop(0)
    dst = refs.pop(0)
    if step is not None:
        full = refs.pop(0)
    if tables:
        synth_ref, analysis_ref = refs.pop(0), refs.pop(0)
    send_sem, recv_sem, ring_send, ring_recv, own_sem = refs

    me = lax.axis_index("space")
    pert = lax.axis_index("pert")
    half, y = pert // 4, lax.rem(pert, 4)
    after, before = half * 4 + lax.rem(y + 1, 4), half * 4 + lax.rem(y + 3, 4)
    barrier = pltpu.get_barrier_semaphore()

    def greet(i, _):
        pl.semaphore_signal(
            barrier, inc=1, device_id={"space": lax.rem(me + i, SPACE)}, device_id_type=MESH
        )
        return 0

    lax.fori_loop(1, SPACE, greet, 0)
    guests = SPACE - 1
    if step is not None:
        for neighbour in (after, before):
            pl.semaphore_signal(barrier, inc=1, device_id={"pert": neighbour}, device_id_type=MESH)
        guests += 2
    pl.semaphore_wait(barrier, guests)

    def copy(i):
        to = lax.rem(me + i, SPACE)
        return remote(src.at[to], dst.at[me], send_sem.at[i], recv_sem.at[i], space=to)

    def start(i, _):
        copy(i).start()
        return 0

    lax.fori_loop(1, SPACE, start, 0)
    local = [pltpu.make_async_copy(src.at[me], dst.at[me], own_sem.at[0])]
    ring = []
    if step is not None:
        blocks = ((own_ref.at[step], half * 4), (part_ref.at[step], (1 - half) * 4))
        for n, (block, group) in enumerate(blocks):
            here = full.at[group + y]
            local.append(pltpu.make_async_copy(block, here, own_sem.at[1 + n]))
            ring.append(remote(block, here, ring_send.at[2 * n], ring_recv.at[2 * n], pert=after))
            ring.append(remote(block, here, ring_send.at[2 * n + 1], ring_recv.at[2 * n + 1], pert=before))
        for c in ring:
            c.start()
    for c in local:
        c.start()
    if tables:
        zonal_tables(wave_ref, synth_ref, analysis_ref)
    passed = []
    if step is not None:
        cut = LATS // 2 + 1
        for n, (_, group) in enumerate(blocks):
            for way, (origin, rows, to) in enumerate((
                (group + lax.rem(y + 3, 4), pl.ds(0, cut), after),
                (group + lax.rem(y + 1, 4), pl.ds(cut, LATS - cut), before),
            )):
                ring[2 * n + way].wait_recv()
                piece = full.at[origin, rows]
                at = 4 + 2 * n + way
                passed.append(remote(piece, piece, ring_send.at[at], ring_recv.at[at], pert=to))
                passed[-1].start()

    def finish(i, _):
        origin = lax.rem(me - i + SPACE, SPACE)
        remote(
            src.at[origin], dst.at[origin], send_sem.at[i], recv_sem.at[i], space=origin
        ).wait_recv()
        copy(i).wait_send()
        return 0

    lax.fori_loop(1, SPACE, finish, 0)
    for c in ring:
        c.wait_send()
    for c in passed:
        c.wait()
    for c in local:
        c.wait()


VMEM = pl.BlockSpec(memory_space=pltpu.VMEM)
SMEM = pl.BlockSpec(memory_space=pltpu.SMEM)
ANY = pl.BlockSpec(memory_space=pl.ANY)
PARAMS = pltpu.CompilerParams(vmem_limit_bytes=56 * 2**20)


def exchange(number, x, step=None, own=None, part=None, wave_rows=None):
    given, in_specs = [x], [ANY]
    out_shape, out_specs = [jax.ShapeDtypeStruct(x.shape, x.dtype)], [ANY]
    if step is not None:
        given += [own, part]
        in_specs += [ANY, ANY]
        out_shape.append(jax.ShapeDtypeStruct((PERT,) + own.shape[1:], BF16))
        out_specs.append(ANY)
    if wave_rows is not None:
        given.append(wave_rows)
        in_specs.append(VMEM)
        out_shape += [jax.ShapeDtypeStruct((2 * M, NLON), BF16)] * 2
        out_specs += [VMEM] * 2
    tables = wave_rows is not None
    return pl.pallas_call(
        lambda *refs: exchange_kernel(step, tables, *refs),
        out_shape=out_shape,
        in_specs=in_specs,
        out_specs=out_specs,
        scratch_shapes=[
            pltpu.SemaphoreType.DMA((SPACE,)),
            pltpu.SemaphoreType.DMA((SPACE,)),
            pltpu.SemaphoreType.DMA((8,)),
            pltpu.SemaphoreType.DMA((8,)),
            pltpu.SemaphoreType.DMA((3,)),
        ],
        compiler_params=pltpu.CompilerParams(collective_id=number, has_side_effects=True),
        name="exchange",
    )(*given)


def grid_stage(weight, wave_rows, rows, synth, analysis, traj):
    whole = lambda shape: pl.BlockSpec(shape, lambda g: (0,) * len(shape), pipeline_mode=pl.Buffered(1))
    return pl.pallas_call(
        grid_kernel,
        grid=(PAD // GROUP,),
        out_shape=jax.ShapeDtypeStruct((M * PAD, COLS), BF16),
        in_specs=[
            SMEM,
            whole((M, 1)),
            whole((M * PAD, COLS)),
            whole((2 * M, NLON)),
            whole((2 * M, NLON)),
            whole((PERT, LATS, 3, 4, NLON)),
        ],
        out_specs=pl.BlockSpec((M * PAD, COLS), lambda g: (0, 0), pipeline_mode=pl.Buffered(1)),
        scratch_shapes=[pltpu.VMEM((M * PAD, COLS), F32), pltpu.VMEM((M * PAD, COLS), F32)],
        compiler_params=PARAMS,
        name="grid_stage",
    )(weight, wave_rows, rows, synth, analysis, traj)


def shards(spectra, wave_order, traj_wind, traj_state, vertical_modes, mode_speeds):
    lat_rows, weight = northern()
    fields = jnp.concatenate([traj_wind[:, None], traj_state], axis=1)
    fields = jnp.transpose(fields, (0, 3, 1, 2, 4))
    partner = lax.ppermute(fields, "pert", [(p, (p + 4) % PERT) for p in range(PERT)])
    wave_rows = wave_order.astype(F32)[:, None]

    send_shape = jax.ShapeDtypeStruct((SPACE, SLOTS, PAD, COLS), BF16)
    state_shape = jax.ShapeDtypeStruct((SLOTS, M, COLS), F32)
    table, state, send, mix, speed = pl.pallas_call(
        table_kernel,
        out_shape=(
            jax.ShapeDtypeStruct((SLOTS, M, HALF), BF16),
            state_shape,
            send_shape,
            jax.ShapeDtypeStruct((2, 2 * COLS, 2 * COLS), BF16),
            jax.ShapeDtypeStruct((8, COLS), F32),
        ),
        in_specs=[SMEM] + [VMEM] * 4,
        out_specs=(VMEM,) * 5,
        scratch_shapes=[pltpu.VMEM((2, 16 * M, 128), F32)],
        compiler_params=PARAMS,
        cost_estimate=pl.CostEstimate(flops=10**10, bytes_accessed=3 * 10**7, transcendentals=10**6),
        name="table_stage",
    )(wave_order, jnp.asarray(lat_rows), spectra, vertical_modes, mode_speeds[None])

    for step in range(STEPS):
        if step == 0:
            rows, traj, synth, analysis = exchange(1, send, 0, fields, partner, wave_rows)
        else:
            rows = exchange(3, send)[0]
        waves = grid_stage(jnp.asarray(weight), wave_rows, rows.reshape(M * PAD, COLS), synth, analysis, traj)
        waves = waves.reshape(SPACE, SLOTS, PAD, COLS)
        if step == 0:
            back, traj = exchange(2, waves, 1, fields, partner)
        else:
            back = exchange(3, waves)[0]
        last = step == STEPS - 1
        result = pl.pallas_call(
            lambda *refs, last=last: update_kernel(last, *refs),
            out_shape=state_shape if last else (state_shape, send_shape),
            in_specs=[SMEM] + [VMEM] * 5,
            out_specs=VMEM if last else (VMEM, VMEM),
            compiler_params=PARAMS,
            name="last_update" if last else "update",
        )(wave_order, table, state, back, mix, speed)
        if last:
            return result
        state, send = result


def solution(mesh):
    placed = (
        P("space", None, "pert"),
        P(),
        P(None, "pert", "space", None),
        P(None, None, "pert", "space", None),
        P(),
        P(),
    )
    return jax.shard_map(
        shards, mesh=mesh, in_specs=placed, out_specs=P("space", None, "pert"), check_vma=False
    )
```

time: 292 us -> 224 us (0.77)
  Pallas kernels: 263 us -> 218 us
  between operations: 13.5 us -> 0.06 us
  local copies, waits for them, and re-layouts: 13.4 us -> 1.65 us
    pallas_call x6 -> x5, Pallas kernels: 200 us -> 171 us  [the longest x4 155 us: exchange(): pl.pallas_call(lambda *refs: exchange_kernel(step, tables, *refs), out_sh...]
    pallas_call x2, Pallas kernels: 36 us -> 20.6 us  [shards(): pl.pallas_call(lambda *refs, last=last: update_kernel(last, *refs), out_s...]
    all_gather x2 -> x0, local copies, waits for them, and re-layouts: 8.98 us -> none  [shards(): gathered.append(lax.all_gather(fields, 'pert', axis=0))]
  transfers between devices with their start and end apart: 2 -> 1, of which waited for: 0 -> 0; matrix products, arithmetic and copies ran while one was open for 3% -> 0% of each run, Pallas kernels for 67% -> 7%
where the time goes in v2:
time: 224 us
  Pallas kernels  218 us (97%)
  starting transfers between devices  2.54 us (1%)
    pallas_call x4, Pallas kernels, exchange(): pl.pallas_call(lambda *refs: exchange_kernel(step, tables, *refs), out_sh...  155 us
    pallas_call x2, Pallas kernels, grid_stage(): pl.pallas_call(grid_kernel, grid=(PAD // GROUP,), out_shape=jax.ShapeDtyp...  26.6 us
    pallas_call x2, Pallas kernels, shards(): pl.pallas_call(lambda *refs, last=last: update_kernel(last, *refs), out_s...  20.6 us
    pallas_call x1, Pallas kernels, shards(): pl.pallas_call(table_kernel, out_shape=(jax.ShapeDtypeStruct((SLOTS, M, H...  15.7 us
  transfers between devices with their start and end apart: 1, of which 0 were waited for; matrix products, arithmetic and copies ran while one was open for 0% of the time, Pallas kernels for 7%

profile of v2, /device:TPU:1, one launch (start us, length us, event | category | flops | bytes accessed | tf_op | source)
XLA Modules:
  0.0 224.0 jit_solution(7799617799953610554)
XLA Ops:
  0.0 0.0 copy-start.2
  0.0 1.5 maximum_bitcast_fusion.refs_1_
  1.5 0.0 copy-start
  1.5 2.5 %collective-permute-start = (bf16[2,15,3,4,960]{4,3,2,1,0:T(4,128)(2,1)S(1)}, bf16[2,15,3,4,960]{4,3,2,1,0:T(4,128)(2,1)S(1)}, u32[]{:S(2)}, u32[]{:S(2)}) collective-permute-start(bf16[2,15,3,4,960]{4,3,2,1,0:T(4,128)(2,1)S(1)} %maximum_bitcast_fusion.refs_1_), channel_id=1, source_target_pairs={{0,128},{32,160},{64,192},{96,224},{128,0},{160,32},{192,64},{224,... | collective-permute-start | bytes 2073608 | tf_op jit(solution)/shard_map/ppermute | solution.py:455
  4.1 0.0 copy-done.2
  4.1 0.8 broadcast_in_dim.12.refs_3_.wave_ref
  4.8 15.7 %table_stage.1 = (bf16[10,320,256]{2,1,0:T(8,128)(2,1)}, f32[10,320,128]{2,1,0:T(8,128)}, bf16[32,10,16,128]{3,2,1,0:T(8,128)(2,1)}, bf16[2,256,256]{2,1,0:T(8,128)(2,1)}, f32[8,128]{1,0:T(8,128)}) custom-call(s32[320]{0:T(512)} %refs_0_.3, f32[3,256]{1,0:T(4,128)} %constant.4.clone.lat_ref, f32[10,320,128]{2,1,0:T(8,128)} %spectra_ref.1, ...), custom_call_target="tpu_custom_call" | custom-call | flops 10000000000 | bytes 30000000 | tf_op jit(solution)/shard_map/table_stage/pallas_call | solution.py:460
  20.5 0.0 copy-done
  20.5 0.0 collective-permute-done.refs_2_
  20.5 0.0 copy-start.1
  20.5 0.9 copy-done.1
  21.4 42.1 %exchange.4 = (bf16[32,10,16,128]{3,2,1,0:T(8,128)(2,1)}, bf16[8,15,3,4,960]{4,3,2,1,0:T(4,128)(2,1)}, bf16[640,960]{1,0:T(8,128)(2,1)}, bf16[640,960]{1,0:T(8,128)(2,1)}) custom-call(bf16[32,10,16,128]{3,2,1,0:T(8,128)(2,1)} %get-tuple-element.20.refs_0_, bf16[2,15,3,4,960]{4,3,2,1,0:T(4,128)(2,1)} %copy-done, bf16[2,15,3,4,960]{4,3,2,1,0:T(4,128)(2,1)} %copy-done.1, ...), custom_call_target="tpu_custom_call" | custom-call | tf_op jit(solution)/shard_map/exchange/pallas_call | solution.py:413
  63.5 13.3 %grid_stage.2 = bf16[5120,128]{1,0:T(8,128)(2,1)} custom-call(f32[240]{0:T(256)} %constant.5.clone.weight_smem, f32[320,1]{1,0:T(8,128)} %broadcast_in_dim.12.refs_3_.wave_ref, bf16[5120,128]{1,0:T(8,128)(2,1)} %bitcast.11, bf16[640,960]{1,0:T(8,128)(2,1)} %get-tuple-element.22.synth_ref, bf16[640,960]{1,0:T(8,128)(2,1)} %get-tuple-element.23.analysis_ref, ...), custom_call_target="tpu_custom_call" | custom-call | tf_op jit(solution)/shard_map/grid_stage/pallas_call | solution.py:432
  76.8 39.3 %exchange.5 = (bf16[32,10,16,128]{3,2,1,0:T(8,128)(2,1)}, bf16[8,15,3,4,960]{4,3,2,1,0:T(4,128)(2,1)}) custom-call(bf16[32,10,16,128]{3,2,1,0:T(8,128)(2,1)} %bitcast.9, bf16[2,15,3,4,960]{4,3,2,1,0:T(4,128)(2,1)} %copy-done, bf16[2,15,3,4,960]{4,3,2,1,0:T(4,128)(2,1)} %copy-done.1), custom_call_target="tpu_custom_call" | custom-call | tf_op jit(solution)/shard_map/exchange/pallas_call | solution.py:413
  116.1 10.9 %update.1 = (f32[10,320,128]{2,1,0:T(8,128)}, bf16[32,10,16,128]{3,2,1,0:T(8,128)(2,1)}) custom-call(s32[320]{0:T(512)} %refs_0_.3, bf16[10,320,256]{2,1,0:T(8,128)(2,1)} %get-tuple-element.18.refs_1_, f32[10,320,128]{2,1,0:T(8,128)} %get-tuple-element.19.refs_2_, bf16[32,10,16,128]{3,2,1,0:T(8,128)(2,1)} %get-tuple-element.25.refs_3_, ...), custom_call_target="tpu_custom_call" | custom-call | tf_op jit(solution)/shard_map/update/pallas_call | solution.py:489
  127.0 36.0 %exchange.6 = bf16[32,10,16,128]{3,2,1,0:T(8,128)(2,1)} custom-call(bf16[32,10,16,128]{3,2,1,0:T(8,128)(2,1)} %get-tuple-element.29.refs_0_), custom_call_target="tpu_custom_call" | custom-call | tf_op jit(solution)/shard_map/exchange/pallas_call | solution.py:413
  163.0 13.3 %grid_stage.3 = bf16[5120,128]{1,0:T(8,128)(2,1)} custom-call(f32[240]{0:T(256)} %constant.5.clone.weight_smem, f32[320,1]{1,0:T(8,128)} %broadcast_in_dim.12.refs_3_.wave_ref, bf16[5120,128]{1,0:T(8,128)(2,1)} %bitcast.8, bf16[640,960]{1,0:T(8,128)(2,1)} %get-tuple-element.22.synth_ref, bf16[640,960]{1,0:T(8,128)(2,1)} %get-tuple-element.23.analysis_ref, ...), custom_call_target="tpu_custom_call" | custom-call | tf_op jit(solution)/shard_map/grid_stage/pallas_call | solution.py:432
  176.3 38.0 %exchange.7.refs_3_ = bf16[32,10,16,128]{3,2,1,0:T(8,128)(2,1)} custom-call(bf16[32,10,16,128]{3,2,1,0:T(8,128)(2,1)} %bitcast.10), custom_call_target="tpu_custom_call" | custom-call | tf_op jit(solution)/shard_map/exchange/pallas_call | solution.py:413
  214.2 9.7 %last_update.1 = f32[10,320,128]{2,1,0:T(8,128)} custom-call(s32[320]{0:T(512)} %refs_0_.3, bf16[10,320,256]{2,1,0:T(8,128)(2,1)} %get-tuple-element.18.refs_1_, f32[10,320,128]{2,1,0:T(8,128)} %get-tuple-element.28.refs_2_, bf16[32,10,16,128]{3,2,1,0:T(8,128)(2,1)} %exchange.7.refs_3_, bf16[2,256,256]{2,1,0:T(8,128)(2,1)} %get-tuple-element.26.refs_4_, ...), custom_call_target="tpu_custom_call" | custom-call | tf_op jit(solution)/shard_map/last_update/pallas_call | solution.py:489
  (1 shorter events, 0.0 us)
Async XLA Ops:
  0.0 4.1 %copy-start.2 = (s32[320]{0:T(512)S(1)}, s32[320]{0:T(512)}, u32[]{:S(2)}) copy-start(s32[320]{0:T(512)} %refs_0_.3) | copy-start | bytes 3844
  1.5 19.0 %copy-start = (bf16[2,15,3,4,960]{4,3,2,1,0:T(4,128)(2,1)}, bf16[2,15,3,4,960]{4,3,2,1,0:T(4,128)(2,1)S(1)}, u32[]{:S(2)}) copy-start(bf16[2,15,3,4,960]{4,3,2,1,0:T(4,128)(2,1)S(1)} %maximum_bitcast_fusion.refs_1_) | copy-start | bytes 2073604
  1.5 19.0 %collective-permute-start = (bf16[2,15,3,4,960]{4,3,2,1,0:T(4,128)(2,1)S(1)}, bf16[2,15,3,4,960]{4,3,2,1,0:T(4,128)(2,1)S(1)}, u32[]{:S(2)}, u32[]{:S(2)}) collective-permute-start(bf16[2,15,3,4,960]{4,3,2,1,0:T(4,128)(2,1)S(1)} %maximum_bitcast_fusion.refs_1_), channel_id=1, source_target_pairs={{0,128},{32,160},{64,192},{96,224},{128,0},{160,32},{192,64},{224,... | collective-permute-start | bytes 2073608 | tf_op jit(solution)/shard_map/ppermute | solution.py:455
  20.5 0.9 copy-start.1

commit v3 on v2

v3 whole, which is shorter than its diff:
```python
import math

import jax
import jax.numpy as jnp
import numpy as np
from jax import lax
from jax.experimental import pallas as pl
from jax.experimental.pallas import tpu as pltpu
from jax.sharding import PartitionSpec as P

NLAT = 480
NLON = 960
M = 320
VARS = 2
LEV = 32
STEPS = 2
PERT = 8
SPACE = 32
SLOTS = M // SPACE
LATS = NLAT // SPACE
PAD = 16
HALF = (SPACE // 2) * PAD
COLS = 128
ROWS = COLS // 2
HK = M // 2
PART = PAD // 2
CHUNKS = 8
GROUP = 4
F32 = jnp.float32
BF16 = jnp.bfloat16
MESH = pl.DeviceIdType.MESH
HIGHEST = lax.Precision.HIGHEST


def dot(a, b, dims=((1,), (0,)), precision=None):
    return lax.dot_general(
        a, b, (dims, ((), ())), preferred_element_type=F32, precision=precision
    )


def iota(shape, axis):
    return lax.broadcasted_iota(jnp.int32, shape, axis)


def level_of(new):
    return new % ROWS // 8 * 4 + new % 4


def group_of(new):
    return new // ROWS * 2 + new % 8 // 4


def reordered(old, new):
    return old == new % 8 // 4 * 64 + level_of(new) * 2 + new // ROWS


def split(x):
    high = x.astype(BF16)
    return jnp.concatenate([high, (x - high.astype(F32)).astype(BF16)], axis=1)


def northern():
    place = np.arange(HALF)
    row = place // COLS * PART + place % PART
    inside = row < LATS
    lat = np.minimum(place % COLS // PART * LATS + row, NLAT // 2 - 1)
    angle = (lat + 0.5) * (math.pi / NLAT)
    rows = np.stack([np.cos(angle), np.log(np.sin(angle)), inside.astype(np.float64)])
    weight = np.sin((np.arange(NLAT // 2) + 0.5) * (math.pi / NLAT)) * (math.pi / NLAT)
    return rows.astype(np.float32), weight.astype(np.float32)


def keep_of(w):
    row = iota((M, COLS), 0)
    degree = jnp.where(row < HK, 2 * row, 2 * row - (M - 1)) + w
    keep = (degree <= M - 1) & jnp.logical_not((iota((M, COLS), 1) >= ROWS) & (w == 0))
    return keep.astype(F32), degree


def legendre_rows(j, table_ref, state, send_ref):
    even, odd = state[:HK], state[HK:]
    both = jnp.concatenate(
        [jnp.concatenate([even, even], axis=1), jnp.concatenate([odd, -odd], axis=1)], axis=0
    )
    rows = dot(table_ref[j], both, ((0,), (0,)))
    for half in range(2):
        for d in range(SPACE // 2):
            at = half * COLS + d * PART
            send_ref[half, d, j] = rows[at : at + PART, :COLS].astype(BF16)
            send_ref[half, SPACE - 1 - d, j] = rows[at : at + PART, COLS:].astype(BF16)


def table_kernel(
    wave_smem, lat_ref, spectra_ref, modes_ref, speeds_ref,
    table_ref, state_ref, send_ref, mix_ref, speed_ref, scratch,
):
    lev = iota((LEV, COLS), 0)
    onehot = (level_of(iota((LEV, COLS), 1)) == lev).astype(F32)
    same = (group_of(iota((COLS, COLS), 0)) == group_of(iota((COLS, COLS), 1))).astype(F32)
    for way in range(2):
        spread = dot(onehot, modes_ref[...], ((0,), (1 - way,)), HIGHEST)
        mix = dot(spread, onehot, precision=HIGHEST) * same
        high = mix.astype(BF16)
        low = (mix - high.astype(F32)).astype(BF16)
        mix_ref[way, :COLS, :COLS] = high
        mix_ref[way, :COLS, COLS:] = low
        mix_ref[way, COLS:, :COLS] = high
        mix_ref[way, COLS:, COLS:] = jnp.zeros_like(low)
    speed_ref[...] = dot(jnp.broadcast_to(speeds_ref[...], (8, LEV)), onehot, precision=HIGHEST)

    base = lax.axis_index("space") * SLOTS
    row16 = iota((16, 128), 0)
    wave = jnp.zeros((16, 128), jnp.int32)
    for j in range(SLOTS):
        wave = jnp.where(row16 == j, wave_smem[base + j], wave)
    wave = wave.astype(F32)
    cosines = [lat_ref[0:1, c * 128 : (c + 1) * 128] for c in range(2)]
    number = (iota((16, 384), 1) + 1).astype(F32)
    terms = jnp.where(number <= wave[:, 0:1], jnp.log((2.0 * number + 1.0) / (2.0 * number)), 0.0)
    start = 0.5 * jnp.sum(terms, axis=1, keepdims=True) - 0.5 * math.log(2.0)
    starts = [start + wave * lat_ref[1:2, c * 128 : (c + 1) * 128] for c in range(2)]
    inside = [lat_ref[2:3, c * 128 : (c + 1) * 128] for c in range(2)]

    def block(b, carry):
        current, previous, logs, last = carry
        current, previous, logs = list(current), list(previous), list(logs)
        factor = [jnp.exp(starts[c] + logs[c]) * inside[c] for c in range(2)]
        first = b * 16
        for i in range(16):
            k = (first + i).astype(F32)
            keep = (wave + k <= M - 1.0).astype(F32)
            row = (i % 2) * HK + b * 8 + i // 2
            for c in range(2):
                scratch[c, pl.ds(row, 16, stride=M), :] = current[c] * (factor[c] * keep)
            up = k + 1.0
            degree2 = 2.0 * (wave + up)
            coef = jnp.sqrt((degree2 * degree2 - 1.0) / (up * (2.0 * wave + up)))
            ratio = coef / last
            for c in range(2):
                following = (coef * cosines[c]) * current[c] - ratio * previous[c]
                previous[c] = current[c]
                current[c] = following
            last = coef
        for c in range(2):
            biggest = jnp.maximum(jnp.abs(current[c]), jnp.abs(previous[c]))
            shrink = 1.0 / biggest
            current[c] = current[c] * shrink
            previous[c] = previous[c] * shrink
            logs[c] = logs[c] + jnp.log(biggest)
        return tuple(current), tuple(previous), tuple(logs), last

    ones = jnp.ones((16, 128), F32)
    zeros = jnp.zeros((16, 128), F32)
    lax.fori_loop(0, M // 16, block, ((ones, ones), (zeros, zeros), (zeros, zeros), ones))

    old, new = iota((2 * COLS, 2 * COLS), 0), iota((2 * COLS, 2 * COLS), 1)
    perm = (reordered(old % COLS, new % COLS) & (old // COLS == new // COLS)).astype(BF16)

    def slot(j, _):
        for c in range(2):
            table_ref[j, :, c * 128 : (c + 1) * 128] = scratch[c, pl.ds(j * M, M), :].astype(BF16)
        keep, _ = keep_of(wave_smem[base + j])
        given = jnp.concatenate(
            [spectra_ref[j, pl.ds(parity, HK, stride=2), :] for parity in range(2)], axis=0
        )
        moved = dot(split(given), perm)
        high = moved[:, :COLS] * keep
        state_ref[j] = high + moved[:, COLS:] * keep
        legendre_rows(j, table_ref, high.astype(BF16), send_ref)
        return 0

    lax.fori_loop(0, SLOTS, slot, 0)


def updated(j, w, table_ref, state_ref, rows_ref, mix_ref, speed):
    sides = []
    for order in (lambda d: d, lambda d: SPACE - 1 - d):
        pieces = [
            rows_ref[half, order(d), j].astype(F32) for half in range(2) for d in range(SPACE // 2)
        ]
        sides.append(jnp.concatenate(pieces, axis=0).astype(BF16))
    change = dot(table_ref[j], jnp.concatenate(sides, axis=1))
    north, south = change[:, :COLS], change[:, COLS:]
    change = jnp.concatenate([north[:HK] + south[:HK], north[HK:] - south[HK:]], axis=0)
    combined = state_ref[j] + change
    keep, degree = keep_of(w)
    stiffness = speed * (degree * (degree + 1)).astype(F32)
    damping = stiffness / (1.0 + stiffness)
    projected = dot(split(combined), mix_ref[0])
    projected = damping * (projected[:, :COLS] + projected[:, COLS:])
    returned = dot(split(projected), mix_ref[1])
    return (combined - (returned[:, :COLS] + returned[:, COLS:])) * keep


def update_kernel(wave_smem, table_ref, state_ref, rows_ref, mix_ref, speed_ref, out_ref):
    base = lax.axis_index("space") * SLOTS
    speed = speed_ref[0:1, :]
    new, old = iota((2 * COLS, COLS), 0), iota((2 * COLS, COLS), 1)
    perm = reordered(old, new % COLS).astype(BF16)

    def slot(j, _):
        result = updated(j, wave_smem[base + j], table_ref, state_ref, rows_ref, mix_ref, speed)
        result = dot(split(result), perm)
        for parity in range(2):
            out_ref[j, pl.ds(parity, HK, stride=2), :] = result[parity * HK : (parity + 1) * HK]
        return 0

    lax.fori_loop(0, SLOTS, slot, 0)


def zonal_tables(wave_ref, synth_ref, analysis_ref):
    step = 2.0 * math.pi / NLON

    def angle_of(count):
        return (count - NLON * jnp.floor(count * (1.0 / NLON))) * step

    def rows(i, _):
        at = pl.ds(pl.multiple_of(i * 64, 64), 64)
        below = pl.ds(pl.multiple_of(M + i * 64, 64), 64)
        wave = wave_ref[at, :]
        x = iota((64, 128), 1).astype(F32)
        angle = angle_of(wave * x)
        turn = angle_of(wave * jnp.full((64, 128), 128.0, F32))
        cosine, sine = jnp.cos(angle), jnp.sin(angle)
        turn_cosine, turn_sine = jnp.cos(turn), jnp.sin(turn)
        factor = jnp.where(wave == 0.0, 1.0, 2.0)
        for c in range(CHUNKS):
            width = min(128, NLON - c * 128)
            lanes = slice(c * 128, c * 128 + width)
            synth_ref[at, lanes] = (factor * cosine)[:, :width].astype(BF16)
            synth_ref[below, lanes] = (-factor * sine)[:, :width].astype(BF16)
            analysis_ref[at, lanes] = (cosine * (1.0 / NLON))[:, :width].astype(BF16)
            analysis_ref[below, lanes] = (sine * (-1.0 / NLON))[:, :width].astype(BF16)
            cosine, sine = (
                cosine * turn_cosine - sine * turn_sine,
                sine * turn_cosine + cosine * turn_sine,
            )
        return 0

    lax.fori_loop(0, M // 64, rows, 0)


def grid_half(half, weight_smem, wave_ref, rows_ref, synth_ref, analysis_ref, traj_ref, out_ref, wide, narrow):
    space = lax.axis_index("space")
    flip = space >= SPACE // 2
    first_weight = jnp.where(flip, SPACE - 1 - space, space) * LATS

    def widen(n, _):
        at = pl.ds(pl.multiple_of(n * (SLOTS * PART), SLOTS * PART), SLOTS * PART)
        wide[at, :] = rows_ref[n].astype(F32).reshape(SLOTS * PART, COLS)
        return 0

    lax.fori_loop(0, SPACE, widen, 0)
    wave = wave_ref[...]
    low = iota((M, COLS), 1) < ROWS

    def group(g, _):
        values_in, slopes_in = [], []
        for pair in range(GROUP // 2):
            t = g * GROUP + 2 * pair
            one = wide[pl.ds(t, M, stride=PART), :]
            two = wide[pl.ds(t + 1, M, stride=PART), :]
            real = jnp.where(low, one, pltpu.roll(two, ROWS, 1))
            imag = jnp.where(low, pltpu.roll(one, ROWS, 1), two)
            values_in.append(jnp.concatenate([real, imag], axis=0).astype(BF16))
            slopes_in.append(jnp.concatenate([-wave * imag, wave * real], axis=0).astype(BF16))
        values = dot(jnp.concatenate(values_in, axis=1), synth_ref[...], ((0,), (0,)))
        slopes = dot(jnp.concatenate(slopes_in, axis=1), synth_ref[...], ((0,), (0,)))
        pieces = []
        for q in range(GROUP):
            i = jnp.minimum(half * PART + g * GROUP + q, LATS - 1)
            t = jnp.where(flip, LATS - 1 - i, i)
            now = traj_ref[:, t].astype(F32)
            wind = jnp.concatenate([now[:, 0], now[:, 0]], axis=1)
            state = jnp.concatenate([now[:, 2], now[:, 1]], axis=1)
            v = values[q * ROWS : (q + 1) * ROWS].reshape(8, 8, NLON)
            s = slopes[q * ROWS : (q + 1) * ROWS].reshape(8, 8, NLON)
            forcing = (wind * s + state * v) * -weight_smem[first_weight + i]
            pieces.append(forcing.reshape(ROWS, NLON).astype(BF16))
        forcing = jnp.concatenate(pieces, axis=0)
        waves = dot(analysis_ref[...], forcing, ((1,), (1,)))
        for pair in range(GROUP // 2):
            t = g * GROUP + 2 * pair
            real = waves[0:M, pair * COLS : (pair + 1) * COLS]
            imag = waves[M : 2 * M, pair * COLS : (pair + 1) * COLS]
            narrow[pl.ds(t, M, stride=PART), :] = jnp.where(low, real, pltpu.roll(imag, ROWS, 1))
            narrow[pl.ds(t + 1, M, stride=PART), :] = jnp.where(low, pltpu.roll(real, ROWS, 1), imag)
        return 0

    lax.fori_loop(0, PART // GROUP, group, 0)

    def shrink(n, _):
        at = pl.ds(pl.multiple_of(n * (SLOTS * PART), SLOTS * PART), SLOTS * PART)
        out_ref[n] = narrow[at, :].reshape(SLOTS, PART, COLS).astype(BF16)
        return 0

    lax.fori_loop(0, SPACE, shrink, 0)


def remote(src, dst, send, recv, **to):
    return pltpu.make_async_remote_copy(
        src, dst, send, recv, device_id=to, device_id_type=MESH
    )


def steps_kernel(
    wave_smem, weight_smem, wave_ref, table_ref, state_ref, mix_ref, speed_ref, first_ref, own_ref, part_ref,
    back_ref, result_ref,
    traj, synth, analysis, there_0, there_1, grid_0, grid_1, back_0, second, wide, narrow,
    send_sem, recv_sem, own_sem, ring_send, ring_recv, ring_own,
):
    me = lax.axis_index("space")
    pert = lax.axis_index("pert")
    side, y = pert // 4, lax.rem(pert, 4)
    after, before = side * 4 + lax.rem(y + 1, 4), side * 4 + lax.rem(y + 3, 4)
    barrier = pltpu.get_barrier_semaphore()

    def greet(i, _):
        pl.semaphore_signal(
            barrier, inc=1, device_id={"space": lax.rem(me + i, SPACE)}, device_id_type=MESH
        )
        return 0

    lax.fori_loop(1, SPACE, greet, 0)
    for neighbour in (after, before):
        pl.semaphore_signal(barrier, inc=1, device_id={"pert": neighbour}, device_id_type=MESH)
    pl.semaphore_wait(barrier, SPACE + 1)

    exchanges = ((first_ref, there_0), (grid_0, back_0), (second, there_1), (grid_1, back_ref))

    def own_copy(e, chunk, half, slots):
        src, dst = exchanges[e]
        return pltpu.make_async_copy(
            src.at[half, me, slots], dst.at[half, me, slots], own_sem.at[e, chunk]
        )

    def push(e, chunk, half, slots=pl.ds(0, SLOTS)):
        src, dst = exchanges[e]

        def start(i, _):
            to = lax.rem(me + i, SPACE)
            remote(
                src.at[half, to, slots], dst.at[half, me, slots],
                send_sem.at[e, chunk], recv_sem.at[e, chunk], space=to,
            ).start()
            return 0

        lax.fori_loop(1, SPACE, start, 0)
        own_copy(e, chunk, half, slots).start()

    def everyone(e, chunk, half, slots):
        src, dst = exchanges[e]
        others = pl.ds(0, SPACE - 1)
        return remote(
            src.at[half, others, slots], dst.at[half, others, slots],
            send_sem.at[e, chunk], recv_sem.at[e, chunk], space=lax.rem(me + 1, SPACE),
        )

    def arrive(e, chunk, half, slots=pl.ds(0, SLOTS)):
        everyone(e, chunk, half, slots).wait_recv()
        own_copy(e, chunk, half, slots).wait()

    def drain(e, chunk, half, slots=pl.ds(0, SLOTS)):
        everyone(e, chunk, half, slots).wait_send()

    for half in range(2):
        push(0, half, half)
    rings, locals_ = [], []
    for step in range(STEPS):
        for n, (block, group) in enumerate(
            ((own_ref.at[step], side * 4), (part_ref.at[step], (1 - side) * 4))
        ):
            here = traj.at[step, group + y]
            locals_.append(pltpu.make_async_copy(block, here, ring_own.at[step, n]))
            for way, to in enumerate((after, before)):
                at = 2 * n + way
                rings.append(remote(block, here, ring_send.at[step, at], ring_recv.at[step, at], pert=to))
    for c in rings + locals_:
        c.start()
    passed = []

    def pass_on(step):
        cut = LATS // 2 + 1
        for n, group in enumerate((side * 4, (1 - side) * 4)):
            for way, (origin, rows, to) in enumerate((
                (group + lax.rem(y + 3, 4), pl.ds(0, cut), after),
                (group + lax.rem(y + 1, 4), pl.ds(cut, LATS - cut), before),
            )):
                rings[4 * step + 2 * n + way].wait_recv()
                piece = traj.at[step, origin, rows]
                at = 4 + 2 * n + way
                passed.append(
                    remote(piece, piece, ring_send.at[step, at], ring_recv.at[step, at], pert=to)
                )
                passed[-1].start()

    zonal_tables(wave_ref, synth, analysis)
    pass_on(0)
    speed = speed_ref[0:1, :]
    base = me * SLOTS

    def slot(j, _):
        result = updated(j, wave_smem[base + j], table_ref, state_ref, back_0, mix_ref, speed)
        result_ref[j] = result
        legendre_rows(j, table_ref, result.astype(BF16), second)
        return 0

    few = SLOTS // 2
    early, late = pl.ds(0, few), pl.ds(few, few)
    for step in range(STEPS):
        rows, out = (there_0, grid_0) if step == 0 else (there_1, grid_1)
        for half in range(2):
            if step == 0:
                arrive(0, half, half)
            else:
                arrive(2, half, half, early)
                arrive(2, 2 + half, half, late)
            if half == 0:
                for c in passed[4 * step :]:
                    c.wait_recv()
                for c in locals_[2 * step : 2 * step + 2]:
                    c.wait()
            grid_half(
                half, weight_smem, wave_ref, rows.at[half], synth, analysis, traj.at[step], out.at[half], wide, narrow
            )
            push(2 * step + 1, half, half)
        if step == 0:
            pass_on(1)
            for half in range(2):
                arrive(1, half, half)
            lax.fori_loop(0, few, slot, 0)
            push(2, 0, 0, early)
            lax.fori_loop(few, SLOTS, slot, 0)
            push(2, 2, 0, late)
            push(2, 1, 1, early)
            push(2, 3, 1, late)
    for half in range(2):
        arrive(3, half, half)
    for e in (0, 1, 3):
        for half in range(2):
            drain(e, half, half)
    for half in range(2):
        drain(2, half, half, early)
        drain(2, 2 + half, half, late)
    for c in rings + passed:
        c.wait_send()


VMEM = pl.BlockSpec(memory_space=pltpu.VMEM)
SMEM = pl.BlockSpec(memory_space=pltpu.SMEM)
ANY = pl.BlockSpec(memory_space=pl.ANY)
PARAMS = pltpu.CompilerParams(vmem_limit_bytes=60 * 2**20)


def shards(spectra, wave_order, traj_wind, traj_state, vertical_modes, mode_speeds):
    lat_rows, weight = northern()
    fields = jnp.concatenate([traj_wind[:, None], traj_state], axis=1)
    fields = jnp.transpose(fields, (0, 3, 1, 2, 4))
    partner = lax.ppermute(fields, "pert", [(p, (p + 4) % PERT) for p in range(PERT)])
    wave_rows = wave_order.astype(F32)[:, None]

    rows_shape = (2, SPACE, SLOTS, PART, COLS)
    send_shape = jax.ShapeDtypeStruct(rows_shape, BF16)
    state_shape = jax.ShapeDtypeStruct((SLOTS, M, COLS), F32)
    table, state, send, mix, speed = pl.pallas_call(
        table_kernel,
        out_shape=(
            jax.ShapeDtypeStruct((SLOTS, M, HALF), BF16),
            state_shape,
            send_shape,
            jax.ShapeDtypeStruct((2, 2 * COLS, 2 * COLS), BF16),
            jax.ShapeDtypeStruct((8, COLS), F32),
        ),
        in_specs=[SMEM] + [VMEM] * 4,
        out_specs=(VMEM,) * 5,
        scratch_shapes=[pltpu.VMEM((2, 16 * M, 128), F32)],
        compiler_params=PARAMS,
        cost_estimate=pl.CostEstimate(flops=10**10, bytes_accessed=3 * 10**7, transcendentals=10**6),
        name="table_stage",
    )(wave_order, jnp.asarray(lat_rows), spectra, vertical_modes, mode_speeds[None])
    back, state = pl.pallas_call(
        steps_kernel,
        out_shape=(send_shape, state_shape),
        in_specs=[SMEM] * 2 + [VMEM] * 5 + [ANY] * 3,
        out_specs=(ANY, VMEM),
        scratch_shapes=[
            pltpu.VMEM((STEPS, PERT, LATS, 3, 4, NLON), BF16),
            pltpu.VMEM((2 * M, NLON), BF16),
            pltpu.VMEM((2 * M, NLON), BF16),
        ]
        + [pltpu.VMEM(rows_shape, BF16)] * 6
        + [pltpu.VMEM((M * PART, COLS), F32)] * 2
        + [pltpu.SemaphoreType.DMA((4, 4))] * 3
        + [pltpu.SemaphoreType.DMA((STEPS, 8))] * 2
        + [pltpu.SemaphoreType.DMA((STEPS, 2))],
        compiler_params=pltpu.CompilerParams(
            collective_id=1, has_side_effects=True, vmem_limit_bytes=60 * 2**20
        ),
        name="steps",
    )(wave_order, jnp.asarray(weight), wave_rows, table, state, mix, speed, send, fields, partner)
    return pl.pallas_call(
        update_kernel,
        out_shape=state_shape,
        in_specs=[SMEM] + [VMEM] * 5,
        out_specs=VMEM,
        compiler_params=PARAMS,
        name="last_update",
    )(wave_order, table, state, back, mix, speed)


def solution(mesh):
    placed = (
        P("space", None, "pert"),
        P(),
        P(None, "pert", "space", None),
        P(None, None, "pert", "space", None),
        P(),
        P(),
    )
    return jax.shard_map(
        shards, mesh=mesh, in_specs=placed, out_specs=P("space", None, "pert"), check_vma=False
    )
```

time: 224 us -> 188 us (0.84)
  Pallas kernels: 218 us -> 182 us
    pallas_call x8 -> x2, Pallas kernels: 203 us -> 166 us  [the longest x1 157 us: shards(): pl.pallas_call(steps_kernel, out_shape=(send_shape, state_shape), in_spec...]
  transfers between devices with their start and end apart: 1 -> 1, of which waited for: 0 -> 0; matrix products, arithmetic and copies ran while one was open for 0% -> 1% of each run, Pallas kernels for 7% -> 8%
where the time goes in v3:
time: 188 us
  Pallas kernels  182 us (97%)
  starting transfers between devices  2.54 us (1%)
  other arithmetic  2.18 us (1%)
    pallas_call x1, Pallas kernels, shards(): pl.pallas_call(steps_kernel, out_shape=(send_shape, state_shape), in_spec...  157 us
    pallas_call x1, Pallas kernels, shards(): pl.pallas_call(table_kernel, out_shape=(jax.ShapeDtypeStruct((SLOTS, M, H...  15.6 us
    pallas_call x1, Pallas kernels, shards(): pl.pallas_call(update_kernel, out_shape=state_shape, in_specs=[SMEM] + [V...  9.73 us
  transfers between devices with their start and end apart: 1, of which 0 were waited for; matrix products, arithmetic and copies ran while one was open for 1% of the time, Pallas kernels for 8%

profile of v3, /device:TPU:1, one launch (start us, length us, event | category | flops | bytes accessed | tf_op | source)
XLA Modules:
  0.0 188.3 jit_solution(15757973916222636388)
XLA Ops:
  0.0 1.5 maximum_bitcast_fusion.own_ref
  1.5 0.0 copy-start
  1.5 2.5 %collective-permute-start = (bf16[2,15,3,4,960]{4,3,2,1,0:T(4,128)(2,1)S(1)}, bf16[2,15,3,4,960]{4,3,2,1,0:T(4,128)(2,1)S(1)}, u32[]{:S(2)}, u32[]{:S(2)}) collective-permute-start(bf16[2,15,3,4,960]{4,3,2,1,0:T(4,128)(2,1)S(1)} %maximum_bitcast_fusion.own_ref), channel_id=1, source_target_pairs={{0,128},{32,160},{64,192},{96,224},{128,0},{160,32},{192,64},{224,... | collective-permute-start | bytes 2073608 | tf_op jit(solution)/shard_map/ppermute | solution.py:459
  4.1 0.7 convert_element_type.3
  4.7 0.8 broadcast_in_dim.12.wave_ref
  5.5 15.6 %table_stage.1 = (bf16[10,320,256]{2,1,0:T(8,128)(2,1)}, f32[10,320,128]{2,1,0:T(8,128)}, bf16[2,32,10,8,128]{4,3,2,1,0:T(8,128)(2,1)}, bf16[2,256,256]{2,1,0:T(8,128)(2,1)}, f32[8,128]{1,0:T(8,128)}) custom-call(s32[320]{0:T(512)} %wave_smem.5, f32[3,256]{1,0:T(4,128)} %constant.4.clone.lat_ref, f32[10,320,128]{2,1,0:T(8,128)} %spectra_ref.1, ...), custom_call_target="tpu_custom_call" | custom-call | flops 10000000000 | bytes 30000000 | tf_op jit(solution)/shard_map/table_stage/pallas_call | solution.py:465
  21.1 0.0 copy-done
  21.1 0.0 collective-permute-done.part_ref
  21.1 0.0 copy-start.1
  21.1 0.9 copy-done.1
  22.0 156.5 %steps.1 = (bf16[2,32,10,8,128]{4,3,2,1,0:T(8,128)(2,1)}, f32[10,320,128]{2,1,0:T(8,128)}) custom-call(s32[320]{0:T(512)} %wave_smem.5, f32[240]{0:T(256)} %constant.5.clone.weight_smem, f32[320,1]{1,0:T(8,128)} %broadcast_in_dim.12.wave_ref, bf16[10,320,256]{2,1,0:T(8,128)(2,1)} %get-tuple-element.12.table_ref, ...), custom_call_target="tpu_custom_call" | custom-call | tf_op jit(solution)/shard_map/steps/pallas_call | solution.py:481
  178.6 9.7 %last_update.1 = f32[10,320,128]{2,1,0:T(8,128)} custom-call(s32[320]{0:T(512)} %wave_smem.5, bf16[10,320,256]{2,1,0:T(8,128)(2,1)} %get-tuple-element.12.table_ref, f32[10,320,128]{2,1,0:T(8,128)} %get-tuple-element.17.state_ref, bf16[2,32,10,8,128]{4,3,2,1,0:T(8,128)(2,1)} %get-tuple-element.18.rows_ref, bf16[2,256,256]{2,1,0:T(8,128)(2,1)} %get-tuple-element.14.mix_ref, ...), custom_call_target="tpu_custom_call" | custom-call | tf_op jit(solution)/shard_map/last_update/pallas_call | solution.py:501
Async XLA Ops:
  1.5 19.6 %copy-start = (bf16[2,15,3,4,960]{4,3,2,1,0:T(4,128)(2,1)}, bf16[2,15,3,4,960]{4,3,2,1,0:T(4,128)(2,1)S(1)}, u32[]{:S(2)}) copy-start(bf16[2,15,3,4,960]{4,3,2,1,0:T(4,128)(2,1)S(1)} %maximum_bitcast_fusion.own_ref) | copy-start | bytes 2073604
  1.5 19.6 %collective-permute-start = (bf16[2,15,3,4,960]{4,3,2,1,0:T(4,128)(2,1)S(1)}, bf16[2,15,3,4,960]{4,3,2,1,0:T(4,128)(2,1)S(1)}, u32[]{:S(2)}, u32[]{:S(2)}) collective-permute-start(bf16[2,15,3,4,960]{4,3,2,1,0:T(4,128)(2,1)S(1)} %maximum_bitcast_fusion.own_ref), channel_id=1, source_target_pairs={{0,128},{32,160},{64,192},{96,224},{128,0},{160,32},{192,64},{224,... | collective-permute-start | bytes 2073608 | tf_op jit(solution)/shard_map/ppermute | solution.py:459
  21.1 0.9 copy-start.1

commit v4 on v3

--- a/solution.py
+++ b/solution.py
@@ -92,7 +92,7 @@
 
 def table_kernel(
     wave_smem, lat_ref, spectra_ref, modes_ref, speeds_ref,
-    table_ref, state_ref, send_ref, mix_ref, speed_ref, scratch,
+    table_ref, state_ref, send_ref, mix_ref, speed_ref, scratch, coefs,
 ):
     lev = iota((LEV, COLS), 0)
     onehot = (level_of(iota((LEV, COLS), 1)) == lev).astype(F32)
@@ -121,42 +121,43 @@
     starts = [start + wave * lat_ref[1:2, c * 128 : (c + 1) * 128] for c in range(2)]
     inside = [lat_ref[2:3, c * 128 : (c + 1) * 128] for c in range(2)]
 
+    def coefficient(up, w):
+        return jnp.sqrt((4.0 * (w + up) * (w + up) - 1.0) / (up * (2.0 * w + up)))
+
+    for c in range(3):
+        up = (iota((16, 128), 1) + (c * 128 + 1)).astype(F32)
+        coefs[0, c] = coefficient(up, wave)
+        coefs[1, c] = coefs[0, c] / coefficient(jnp.maximum(up - 1.0, 1.0), wave)
+
     def block(b, carry):
-        current, previous, logs, last = carry
-        current, previous, logs = list(current), list(previous), list(logs)
+        current, previous, logs = (list(x) for x in carry)
         factor = [jnp.exp(starts[c] + logs[c]) * inside[c] for c in range(2)]
-        first = b * 16
+        shift = lax.rem(128 - 16 * lax.rem(b, 8), 128)
+        coef, ratio = (pltpu.roll(coefs[n, b // 8], shift, 1) for n in range(2))
         for i in range(16):
-            k = (first + i).astype(F32)
-            keep = (wave + k <= M - 1.0).astype(F32)
             row = (i % 2) * HK + b * 8 + i // 2
+            up, down = (jnp.broadcast_to(x[:, i : i + 1], (16, 128)) for x in (coef, ratio))
             for c in range(2):
-                scratch[c, pl.ds(row, 16, stride=M), :] = current[c] * (factor[c] * keep)
-            up = k + 1.0
-            degree2 = 2.0 * (wave + up)
-            coef = jnp.sqrt((degree2 * degree2 - 1.0) / (up * (2.0 * wave + up)))
-            ratio = coef / last
-            for c in range(2):
-                following = (coef * cosines[c]) * current[c] - ratio * previous[c]
+                scratch[c, pl.ds(row, 16, stride=M), :] = current[c] * factor[c]
+                following = (up * cosines[c]) * current[c] - down * previous[c]
                 previous[c] = current[c]
                 current[c] = following
-            last = coef
         for c in range(2):
             biggest = jnp.maximum(jnp.abs(current[c]), jnp.abs(previous[c]))
             shrink = 1.0 / biggest
             current[c] = current[c] * shrink
             previous[c] = previous[c] * shrink
             logs[c] = logs[c] + jnp.log(biggest)
-        return tuple(current), tuple(previous), tuple(logs), last
+        return tuple(current), tuple(previous), tuple(logs)
 
     ones = jnp.ones((16, 128), F32)
     zeros = jnp.zeros((16, 128), F32)
-    lax.fori_loop(0, M // 16, block, ((ones, ones), (zeros, zeros), (zeros, zeros), ones))
+    lax.fori_loop(0, M // 16, block, ((ones, ones), (zeros, zeros), (zeros, zeros)))
 
     old, new = iota((2 * COLS, 2 * COLS), 0), iota((2 * COLS, 2 * COLS), 1)
     perm = (reordered(old % COLS, new % COLS) & (old // COLS == new // COLS)).astype(BF16)
 
-    def slot(j, _):
+    def slot(j):
         for c in range(2):
             table_ref[j, :, c * 128 : (c + 1) * 128] = scratch[c, pl.ds(j * M, M), :].astype(BF16)
         keep, _ = keep_of(wave_smem[base + j])
@@ -167,9 +168,13 @@
         high = moved[:, :COLS] * keep
         state_ref[j] = high + moved[:, COLS:] * keep
         legendre_rows(j, table_ref, high.astype(BF16), send_ref)
+
+    def pair(n, _):
+        slot(2 * n)
+        slot(2 * n + 1)
         return 0
 
-    lax.fori_loop(0, SLOTS, slot, 0)
+    lax.fori_loop(0, SLOTS // 2, pair, 0)
 
 
 def updated(j, w, table_ref, state_ref, rows_ref, mix_ref, speed):
@@ -190,22 +195,6 @@
     projected = damping * (projected[:, :COLS] + projected[:, COLS:])
     returned = dot(split(projected), mix_ref[1])
     return (combined - (returned[:, :COLS] + returned[:, COLS:])) * keep
-
-
-def update_kernel(wave_smem, table_ref, state_ref, rows_ref, mix_ref, speed_ref, out_ref):
-    base = lax.axis_index("space") * SLOTS
-    speed = speed_ref[0:1, :]
-    new, old = iota((2 * COLS, COLS), 0), iota((2 * COLS, COLS), 1)
-    perm = reordered(old, new % COLS).astype(BF16)
-
-    def slot(j, _):
-        result = updated(j, wave_smem[base + j], table_ref, state_ref, rows_ref, mix_ref, speed)
-        result = dot(split(result), perm)
-        for parity in range(2):
-            out_ref[j, pl.ds(parity, HK, stride=2), :] = result[parity * HK : (parity + 1) * HK]
-        return 0
-
-    lax.fori_loop(0, SLOTS, slot, 0)
 
 
 def zonal_tables(wave_ref, synth_ref, analysis_ref):
@@ -305,8 +294,8 @@
 
 def steps_kernel(
     wave_smem, weight_smem, wave_ref, table_ref, state_ref, mix_ref, speed_ref, first_ref, own_ref, part_ref,
-    back_ref, result_ref,
-    traj, synth, analysis, there_0, there_1, grid_0, grid_1, back_0, second, wide, narrow,
+    out_ref,
+    traj, synth, analysis, there_0, there_1, grid_0, grid_1, back_0, back_1, second, middle, wide, narrow,
     send_sem, recv_sem, own_sem, ring_send, ring_recv, ring_own,
 ):
     me = lax.axis_index("space")
@@ -326,7 +315,7 @@
         pl.semaphore_signal(barrier, inc=1, device_id={"pert": neighbour}, device_id_type=MESH)
     pl.semaphore_wait(barrier, SPACE + 1)
 
-    exchanges = ((first_ref, there_0), (grid_0, back_0), (second, there_1), (grid_1, back_ref))
+    exchanges = ((first_ref, there_0), (grid_0, back_0), (second, there_1), (grid_1, back_1))
 
     def own_copy(e, chunk, half, slots):
         src, dst = exchanges[e]
@@ -399,16 +388,26 @@
     speed = speed_ref[0:1, :]
     base = me * SLOTS
 
-    def slot(j, _):
-        result = updated(j, wave_smem[base + j], table_ref, state_ref, back_0, mix_ref, speed)
-        result_ref[j] = result
-        legendre_rows(j, table_ref, result.astype(BF16), second)
-        return 0
+    new, old = iota((2 * COLS, COLS), 0), iota((2 * COLS, COLS), 1)
+    perm = reordered(old, new % COLS).astype(BF16)
+
+    def slot(step, j):
+        w = wave_smem[base + j]
+        if step == 0:
+            result = updated(j, w, table_ref, state_ref, back_0, mix_ref, speed)
+            middle[j] = result
+            legendre_rows(j, table_ref, result.astype(BF16), second)
+        else:
+            result = updated(j, w, table_ref, middle, back_1, mix_ref, speed)
+            result = dot(split(result), perm)
+            for parity in range(2):
+                out_ref[j, pl.ds(parity, HK, stride=2), :] = result[parity * HK : (parity + 1) * HK]
 
     few = SLOTS // 2
     early, late = pl.ds(0, few), pl.ds(few, few)
     for step in range(STEPS):
         rows, out = (there_0, grid_0) if step == 0 else (there_1, grid_1)
+        back = 2 * step + 1
         for half in range(2):
             if step == 0:
                 arrive(0, half, half)
@@ -423,25 +422,34 @@
             grid_half(
                 half, weight_smem, wave_ref, rows.at[half], synth, analysis, traj.at[step], out.at[half], wide, narrow
             )
-            push(2 * step + 1, half, half)
+            if half == 0:
+                push(back, 0, 0)
+            else:
+                push(back, 1, 1, early)
+                push(back, 2, 1, late)
         if step == 0:
             pass_on(1)
-            for half in range(2):
-                arrive(1, half, half)
-            lax.fori_loop(0, few, slot, 0)
+        arrive(back, 0, 0)
+        arrive(back, 1, 1, early)
+        for j in range(few):
+            slot(step, j)
+        if step == 0:
             push(2, 0, 0, early)
-            lax.fori_loop(few, SLOTS, slot, 0)
+        arrive(back, 2, 1, late)
+        for j in range(few, SLOTS):
+            slot(step, j)
+        if step == 0:
             push(2, 2, 0, late)
             push(2, 1, 1, early)
             push(2, 3, 1, late)
     for half in range(2):
-        arrive(3, half, half)
-    for e in (0, 1, 3):
-        for half in range(2):
-            drain(e, half, half)
-    for half in range(2):
+        drain(0, half, half)
         drain(2, half, half, early)
         drain(2, 2 + half, half, late)
+    for e in (1, 3):
+        drain(e, 0, 0)
+        drain(e, 1, 1, early)
+        drain(e, 2, 1, late)
     for c in rings + passed:
         c.wait_send()
 
@@ -473,22 +481,23 @@
         ),
         in_specs=[SMEM] + [VMEM] * 4,
         out_specs=(VMEM,) * 5,
-        scratch_shapes=[pltpu.VMEM((2, 16 * M, 128), F32)],
+        scratch_shapes=[pltpu.VMEM((2, 16 * M, 128), F32), pltpu.VMEM((2, 3, 16, 128), F32)],
         compiler_params=PARAMS,
         cost_estimate=pl.CostEstimate(flops=10**10, bytes_accessed=3 * 10**7, transcendentals=10**6),
         name="table_stage",
     )(wave_order, jnp.asarray(lat_rows), spectra, vertical_modes, mode_speeds[None])
-    back, state = pl.pallas_call(
+    return pl.pallas_call(
         steps_kernel,
-        out_shape=(send_shape, state_shape),
+        out_shape=state_shape,
         in_specs=[SMEM] * 2 + [VMEM] * 5 + [ANY] * 3,
-        out_specs=(ANY, VMEM),
+        out_specs=VMEM,
         scratch_shapes=[
             pltpu.VMEM((STEPS, PERT, LATS, 3, 4, NLON), BF16),
             pltpu.VMEM((2 * M, NLON), BF16),
             pltpu.VMEM((2 * M, NLON), BF16),
         ]
-        + [pltpu.VMEM(rows_shape, BF16)] * 6
+        + [pltpu.VMEM(rows_shape, BF16)] * 7
+        + [pltpu.VMEM((SLOTS, M, COLS), F32)]
         + [pltpu.VMEM((M * PART, COLS), F32)] * 2
         + [pltpu.SemaphoreType.DMA((4, 4))] * 3
         + [pltpu.SemaphoreType.DMA((STEPS, 8))] * 2
@@ -498,14 +507,6 @@
         ),
         name="steps",
     )(wave_order, jnp.asarray(weight), wave_rows, table, state, mix, speed, send, fields, partner)
-    return pl.pallas_call(
-        update_kernel,
-        out_shape=state_shape,
-        in_specs=[SMEM] + [VMEM] * 5,
-        out_specs=VMEM,
-        compiler_params=PARAMS,
-        name="last_update",
-    )(wave_order, table, state, back, mix, speed)
 
 
 def solution(mesh):

time: 188 us -> 180 us (0.957)
  Pallas kernels: 182 us -> 170 us
  local copies, waits for them, and re-layouts: 1.63 us -> 4.4 us
    pallas_call x2 -> x1, Pallas kernels: 166 us -> 154 us  [shards(): pl.pallas_call(steps_kernel, out_shape=state_shape, in_specs=[SMEM] * 2 +...]
    unnamed x4 -> x5, local copies, waits for them, and re-layouts: 0.88 us -> 3.62 us
  transfers between devices with their start and end apart: 1 -> 1, of which waited for: 0 -> 0; matrix products, arithmetic and copies ran while one was open for 1% -> 1% of each run, Pallas kernels for 8% -> 9%
where the time goes in v4:
time: 180 us; the launch traced here: 179 us
  Pallas kernels  170 us (94%)
  local copies, waits for them, and re-layouts  4.4 us (2%)
  starting transfers between devices  2.54 us (1%)
  other arithmetic  2.18 us (1%)
    pallas_call x1, Pallas kernels, shards(): pl.pallas_call(steps_kernel, out_shape=state_shape, in_specs=[SMEM] * 2 +...  154 us
    pallas_call x1, Pallas kernels, shards(): pl.pallas_call(table_kernel, out_shape=(jax.ShapeDtypeStruct((SLOTS, M, H...  15.9 us
    unnamed x5, local copies, waits for them, and re-layouts  3.62 us
  transfers between devices with their start and end apart: 1, of which 0 were waited for; matrix products, arithmetic and copies ran while one was open for 1% of the time, Pallas kernels for 9%

profile of v4, /device:TPU:1, one launch (start us, length us, event | category | flops | bytes accessed | tf_op | source)
XLA Modules:
  0.0 179.3 jit_solution(16208167947064319474)
XLA Ops:
  0.0 1.5 maximum_bitcast_fusion.own_ref
  1.5 0.0 copy-start
  1.5 2.5 %collective-permute-start = (bf16[2,15,3,4,960]{4,3,2,1,0:T(4,128)(2,1)S(1)}, bf16[2,15,3,4,960]{4,3,2,1,0:T(4,128)(2,1)S(1)}, u32[]{:S(2)}, u32[]{:S(2)}) collective-permute-start(bf16[2,15,3,4,960]{4,3,2,1,0:T(4,128)(2,1)S(1)} %maximum_bitcast_fusion.own_ref), channel_id=1, source_target_pairs={{0,128},{32,160},{64,192},{96,224},{128,0},{160,32},{192,64},{224,... | collective-permute-start | bytes 2073608 | tf_op jit(solution)/shard_map/ppermute | solution.py:467
  4.1 0.7 convert_element_type.3
  4.7 0.8 broadcast_in_dim.12.wave_ref
  5.5 15.9 %table_stage.1 = (bf16[10,320,256]{2,1,0:T(8,128)(2,1)}, f32[10,320,128]{2,1,0:T(8,128)}, bf16[2,32,10,8,128]{4,3,2,1,0:T(8,128)(2,1)}, bf16[2,256,256]{2,1,0:T(8,128)(2,1)}, f32[8,128]{1,0:T(8,128)}) custom-call(s32[320]{0:T(512)} %wave_smem.3, f32[3,256]{1,0:T(4,128)} %constant.4.clone.lat_ref, f32[10,320,128]{2,1,0:T(8,128)} %spectra_ref.1, ...), custom_call_target="tpu_custom_call" | custom-call | flops 10000000000 | bytes 30000000 | tf_op jit(solution)/shard_map/table_stage/pallas_call | solution.py:473
  21.4 0.0 copy-done
  21.4 0.0 collective-permute-done.part_ref
  21.4 0.0 copy-start.1
  21.4 0.9 copy-done.1
  22.3 154.2 %steps.1 = f32[10,320,128]{2,1,0:T(8,128)} custom-call(s32[320]{0:T(512)} %wave_smem.3, f32[240]{0:T(256)} %constant.5.clone.weight_smem, f32[320,1]{1,0:T(8,128)} %broadcast_in_dim.12.wave_ref, bf16[10,320,256]{2,1,0:T(8,128)(2,1)} %get-tuple-element.10.table_ref, f32[10,320,128]{2,1,0:T(8,128)} %get-tuple-element.11.state_ref, ...), custom_call_target="tpu_custom_call" | custom-call | tf_op jit(solution)/shard_map/steps/pallas_call | solution.py:489
  176.6 2.7 %copy.15 = f32[10,320,128]{2,1,0:T(8,128)} copy(f32[10,320,128]{2,1,0:T(8,128)} %steps.1) | data formatting | bytes 3276800
Async XLA Ops:
  1.5 19.9 %copy-start = (bf16[2,15,3,4,960]{4,3,2,1,0:T(4,128)(2,1)}, bf16[2,15,3,4,960]{4,3,2,1,0:T(4,128)(2,1)S(1)}, u32[]{:S(2)}) copy-start(bf16[2,15,3,4,960]{4,3,2,1,0:T(4,128)(2,1)S(1)} %maximum_bitcast_fusion.own_ref) | copy-start | bytes 2073604
  1.5 19.9 %collective-permute-start = (bf16[2,15,3,4,960]{4,3,2,1,0:T(4,128)(2,1)S(1)}, bf16[2,15,3,4,960]{4,3,2,1,0:T(4,128)(2,1)S(1)}, u32[]{:S(2)}, u32[]{:S(2)}) collective-permute-start(bf16[2,15,3,4,960]{4,3,2,1,0:T(4,128)(2,1)S(1)} %maximum_bitcast_fusion.own_ref), channel_id=1, source_target_pairs={{0,128},{32,160},{64,192},{96,224},{128,0},{160,32},{192,64},{224,... | collective-permute-start | bytes 2073608 | tf_op jit(solution)/shard_map/ppermute | solution.py:467
  21.4 0.9 copy-start.1

commit v5 on v4

--- a/solution.py
+++ b/solution.py
@@ -23,6 +23,7 @@
 COLS = 128
 ROWS = COLS // 2
 HK = M // 2
+APART = M + 8
 PART = PAD // 2
 CHUNKS = 8
 GROUP = 4
@@ -90,10 +91,7 @@
             send_ref[half, SPACE - 1 - d, j] = rows[at : at + PART, COLS:].astype(BF16)
 
 
-def table_kernel(
-    wave_smem, lat_ref, spectra_ref, modes_ref, speeds_ref,
-    table_ref, state_ref, send_ref, mix_ref, speed_ref, scratch, coefs,
-):
+def implicit_operators(modes_ref, speeds_ref, mix_ref, speed_ref):
     lev = iota((LEV, COLS), 0)
     onehot = (level_of(iota((LEV, COLS), 1)) == lev).astype(F32)
     same = (group_of(iota((COLS, COLS), 0)) == group_of(iota((COLS, COLS), 1))).astype(F32)
@@ -108,6 +106,8 @@
         mix_ref[way, COLS:, COLS:] = jnp.zeros_like(low)
     speed_ref[...] = dot(jnp.broadcast_to(speeds_ref[...], (8, LEV)), onehot, precision=HIGHEST)
 
+
+def recurrence(wave_smem, lat_ref, scratch, coefs, between):
     base = lax.axis_index("space") * SLOTS
     row16 = iota((16, 128), 0)
     wave = jnp.zeros((16, 128), jnp.int32)
@@ -138,7 +138,7 @@
             row = (i % 2) * HK + b * 8 + i // 2
             up, down = (jnp.broadcast_to(x[:, i : i + 1], (16, 128)) for x in (coef, ratio))
             for c in range(2):
-                scratch[c, pl.ds(row, 16, stride=M), :] = current[c] * factor[c]
+                scratch[c, pl.ds(row, 16, stride=APART), :] = current[c] * factor[c]
                 following = (up * cosines[c]) * current[c] - down * previous[c]
                 previous[c] = current[c]
                 current[c] = following
@@ -152,29 +152,24 @@
 
     ones = jnp.ones((16, 128), F32)
     zeros = jnp.zeros((16, 128), F32)
-    lax.fori_loop(0, M // 16, block, ((ones, ones), (zeros, zeros), (zeros, zeros)))
-
+    half_way = lax.fori_loop(0, M // 32, block, ((ones, ones), (zeros, zeros), (zeros, zeros)))
+    between()
+    lax.fori_loop(M // 32, M // 16, block, half_way)
+
+
+def first_rows(j, w, spectra_ref, scratch, table_ref, state_ref, send_ref):
     old, new = iota((2 * COLS, 2 * COLS), 0), iota((2 * COLS, 2 * COLS), 1)
     perm = (reordered(old % COLS, new % COLS) & (old // COLS == new // COLS)).astype(BF16)
-
-    def slot(j):
-        for c in range(2):
-            table_ref[j, :, c * 128 : (c + 1) * 128] = scratch[c, pl.ds(j * M, M), :].astype(BF16)
-        keep, _ = keep_of(wave_smem[base + j])
-        given = jnp.concatenate(
-            [spectra_ref[j, pl.ds(parity, HK, stride=2), :] for parity in range(2)], axis=0
-        )
-        moved = dot(split(given), perm)
-        high = moved[:, :COLS] * keep
-        state_ref[j] = high + moved[:, COLS:] * keep
-        legendre_rows(j, table_ref, high.astype(BF16), send_ref)
-
-    def pair(n, _):
-        slot(2 * n)
-        slot(2 * n + 1)
-        return 0
-
-    lax.fori_loop(0, SLOTS // 2, pair, 0)
+    for c in range(2):
+        table_ref[j, :, c * 128 : (c + 1) * 128] = scratch[c, pl.ds(j * APART, M), :].astype(BF16)
+    keep, _ = keep_of(w)
+    given = jnp.concatenate(
+        [spectra_ref[j, pl.ds(parity, HK, stride=2), :] for parity in range(2)], axis=0
+    )
+    moved = dot(split(given), perm)
+    high = moved[:, :COLS] * keep
+    state_ref[j] = high + moved[:, COLS:] * keep
+    legendre_rows(j, table_ref, high.astype(BF16), send_ref)
 
 
 def updated(j, w, table_ref, state_ref, rows_ref, mix_ref, speed):
@@ -206,7 +201,7 @@
     def rows(i, _):
         at = pl.ds(pl.multiple_of(i * 64, 64), 64)
         below = pl.ds(pl.multiple_of(M + i * 64, 64), 64)
-        wave = wave_ref[at, :]
+        wave = wave_ref[at, :].astype(F32)
         x = iota((64, 128), 1).astype(F32)
         angle = angle_of(wave * x)
         turn = angle_of(wave * jnp.full((64, 128), 128.0, F32))
@@ -240,7 +235,7 @@
         return 0
 
     lax.fori_loop(0, SPACE, widen, 0)
-    wave = wave_ref[...]
+    wave = wave_ref[...].astype(F32)
     low = iota((M, COLS), 1) < ROWS
 
     def group(g, _):
@@ -293,10 +288,11 @@
 
 
 def steps_kernel(
-    wave_smem, weight_smem, wave_ref, table_ref, state_ref, mix_ref, speed_ref, first_ref, own_ref, part_ref,
+    wave_smem, weight_smem, wave_ref, lat_ref, spectra_ref, modes_ref, speeds_ref, own_ref,
     out_ref,
+    part, scratch, coefs, table_ref, state_ref, mix_ref, speed_ref, first_ref,
     traj, synth, analysis, there_0, there_1, grid_0, grid_1, back_0, back_1, second, middle, wide, narrow,
-    send_sem, recv_sem, own_sem, ring_send, ring_recv, ring_own,
+    send_sem, recv_sem, own_sem, ring_send, ring_recv, ring_own, part_send, part_recv,
 ):
     me = lax.axis_index("space")
     pert = lax.axis_index("pert")
@@ -311,9 +307,9 @@
         return 0
 
     lax.fori_loop(1, SPACE, greet, 0)
-    for neighbour in (after, before):
+    partner = lax.rem(pert + 4, PERT)
+    for neighbour in (after, before, partner):
         pl.semaphore_signal(barrier, inc=1, device_id={"pert": neighbour}, device_id_type=MESH)
-    pl.semaphore_wait(barrier, SPACE + 1)
 
     exchanges = ((first_ref, there_0), (grid_0, back_0), (second, there_1), (grid_1, back_1))
 
@@ -352,20 +348,49 @@
     def drain(e, chunk, half, slots=pl.ds(0, SLOTS)):
         everyone(e, chunk, half, slots).wait_send()
 
-    for half in range(2):
-        push(0, half, half)
-    rings, locals_ = [], []
+    crossing = [
+        remote(own_ref.at[step], part.at[step], part_send.at[step], part_recv.at[step], pert=partner)
+        for step in range(STEPS)
+    ]
+    rings, locals_ = {}, {}
     for step in range(STEPS):
         for n, (block, group) in enumerate(
-            ((own_ref.at[step], side * 4), (part_ref.at[step], (1 - side) * 4))
+            ((own_ref.at[step], side * 4), (part.at[step], (1 - side) * 4))
         ):
             here = traj.at[step, group + y]
-            locals_.append(pltpu.make_async_copy(block, here, ring_own.at[step, n]))
+            locals_[step, n] = pltpu.make_async_copy(block, here, ring_own.at[step, n])
             for way, to in enumerate((after, before)):
                 at = 2 * n + way
-                rings.append(remote(block, here, ring_send.at[step, at], ring_recv.at[step, at], pert=to))
-    for c in rings + locals_:
-        c.start()
+                rings[step, at] = remote(
+                    block, here, ring_send.at[step, at], ring_recv.at[step, at], pert=to
+                )
+
+    def send_round(step, n):
+        locals_[step, n].start()
+        for way in range(2):
+            rings[step, 2 * n + way].start()
+
+    def between():
+        pl.semaphore_wait(barrier, SPACE + 2)
+        for step in range(STEPS):
+            crossing[step].start()
+        for step in range(STEPS):
+            send_round(step, 0)
+
+    recurrence(wave_smem, lat_ref, scratch, coefs, between)
+    base = me * SLOTS
+    few = SLOTS // 2
+    early, late = pl.ds(0, few), pl.ds(few, few)
+    for j in range(SLOTS):
+        first_rows(j, wave_smem[base + j], spectra_ref, scratch, table_ref, state_ref, first_ref)
+        if j == few - 1:
+            push(0, 0, 0, early)
+    push(0, 2, 0, late)
+    push(0, 1, 1, early)
+    push(0, 3, 1, late)
+    crossing[0].wait_recv()
+    send_round(0, 1)
+    implicit_operators(modes_ref, speeds_ref, mix_ref, speed_ref)
     passed = []
 
     def pass_on(step):
@@ -375,7 +400,7 @@
                 (group + lax.rem(y + 3, 4), pl.ds(0, cut), after),
                 (group + lax.rem(y + 1, 4), pl.ds(cut, LATS - cut), before),
             )):
-                rings[4 * step + 2 * n + way].wait_recv()
+                rings[step, 2 * n + way].wait_recv()
                 piece = traj.at[step, origin, rows]
                 at = 4 + 2 * n + way
                 passed.append(
@@ -384,9 +409,10 @@
                 passed[-1].start()
 
     zonal_tables(wave_ref, synth, analysis)
+    crossing[1].wait_recv()
+    send_round(1, 1)
     pass_on(0)
     speed = speed_ref[0:1, :]
-    base = me * SLOTS
 
     new, old = iota((2 * COLS, COLS), 0), iota((2 * COLS, COLS), 1)
     perm = reordered(old, new % COLS).astype(BF16)
@@ -403,22 +429,17 @@
             for parity in range(2):
                 out_ref[j, pl.ds(parity, HK, stride=2), :] = result[parity * HK : (parity + 1) * HK]
 
-    few = SLOTS // 2
-    early, late = pl.ds(0, few), pl.ds(few, few)
     for step in range(STEPS):
         rows, out = (there_0, grid_0) if step == 0 else (there_1, grid_1)
         back = 2 * step + 1
         for half in range(2):
-            if step == 0:
-                arrive(0, half, half)
-            else:
-                arrive(2, half, half, early)
-                arrive(2, 2 + half, half, late)
+            arrive(2 * step, half, half, early)
+            arrive(2 * step, 2 + half, half, late)
             if half == 0:
                 for c in passed[4 * step :]:
                     c.wait_recv()
-                for c in locals_[2 * step : 2 * step + 2]:
-                    c.wait()
+                for n in range(2):
+                    locals_[step, n].wait()
             grid_half(
                 half, weight_smem, wave_ref, rows.at[half], synth, analysis, traj.at[step], out.at[half], wide, narrow
             )
@@ -442,56 +463,42 @@
             push(2, 2, 0, late)
             push(2, 1, 1, early)
             push(2, 3, 1, late)
-    for half in range(2):
-        drain(0, half, half)
-        drain(2, half, half, early)
-        drain(2, 2 + half, half, late)
+    for e in (0, 2):
+        for half in range(2):
+            drain(e, half, half, early)
+            drain(e, 2 + half, half, late)
     for e in (1, 3):
         drain(e, 0, 0)
         drain(e, 1, 1, early)
         drain(e, 2, 1, late)
-    for c in rings + passed:
+    for c in list(rings.values()) + passed + crossing:
         c.wait_send()
 
 
 VMEM = pl.BlockSpec(memory_space=pltpu.VMEM)
 SMEM = pl.BlockSpec(memory_space=pltpu.SMEM)
 ANY = pl.BlockSpec(memory_space=pl.ANY)
-PARAMS = pltpu.CompilerParams(vmem_limit_bytes=60 * 2**20)
 
 
 def shards(spectra, wave_order, traj_wind, traj_state, vertical_modes, mode_speeds):
     lat_rows, weight = northern()
     fields = jnp.concatenate([traj_wind[:, None], traj_state], axis=1)
     fields = jnp.transpose(fields, (0, 3, 1, 2, 4))
-    partner = lax.ppermute(fields, "pert", [(p, (p + 4) % PERT) for p in range(PERT)])
-    wave_rows = wave_order.astype(F32)[:, None]
-
     rows_shape = (2, SPACE, SLOTS, PART, COLS)
-    send_shape = jax.ShapeDtypeStruct(rows_shape, BF16)
-    state_shape = jax.ShapeDtypeStruct((SLOTS, M, COLS), F32)
-    table, state, send, mix, speed = pl.pallas_call(
-        table_kernel,
-        out_shape=(
-            jax.ShapeDtypeStruct((SLOTS, M, HALF), BF16),
-            state_shape,
-            send_shape,
-            jax.ShapeDtypeStruct((2, 2 * COLS, 2 * COLS), BF16),
-            jax.ShapeDtypeStruct((8, COLS), F32),
-        ),
-        in_specs=[SMEM] + [VMEM] * 4,
-        out_specs=(VMEM,) * 5,
-        scratch_shapes=[pltpu.VMEM((2, 16 * M, 128), F32), pltpu.VMEM((2, 3, 16, 128), F32)],
-        compiler_params=PARAMS,
-        cost_estimate=pl.CostEstimate(flops=10**10, bytes_accessed=3 * 10**7, transcendentals=10**6),
-        name="table_stage",
-    )(wave_order, jnp.asarray(lat_rows), spectra, vertical_modes, mode_speeds[None])
     return pl.pallas_call(
         steps_kernel,
-        out_shape=state_shape,
-        in_specs=[SMEM] * 2 + [VMEM] * 5 + [ANY] * 3,
+        out_shape=jax.ShapeDtypeStruct((SLOTS, M, COLS), F32),
+        in_specs=[SMEM] * 2 + [VMEM] * 5 + [ANY],
         out_specs=VMEM,
         scratch_shapes=[
+            pltpu.VMEM(fields.shape, BF16),
+            pltpu.VMEM((2, 16 * APART, 128), F32),
+            pltpu.VMEM((2, 3, 16, 128), F32),
+            pltpu.VMEM((SLOTS, M, HALF), BF16),
+            pltpu.VMEM((SLOTS, M, COLS), F32),
+            pltpu.VMEM((2, 2 * COLS, 2 * COLS), BF16),
+            pltpu.VMEM((8, COLS), F32),
+            pltpu.VMEM(rows_shape, BF16),
             pltpu.VMEM((STEPS, PERT, LATS, 3, 4, NLON), BF16),
             pltpu.VMEM((2 * M, NLON), BF16),
             pltpu.VMEM((2 * M, NLON), BF16),
@@ -501,12 +508,16 @@
         + [pltpu.VMEM((M * PART, COLS), F32)] * 2
         + [pltpu.SemaphoreType.DMA((4, 4))] * 3
         + [pltpu.SemaphoreType.DMA((STEPS, 8))] * 2
-        + [pltpu.SemaphoreType.DMA((STEPS, 2))],
+        + [pltpu.SemaphoreType.DMA((STEPS, 2))]
+        + [pltpu.SemaphoreType.DMA((STEPS,))] * 2,
         compiler_params=pltpu.CompilerParams(
             collective_id=1, has_side_effects=True, vmem_limit_bytes=60 * 2**20
         ),
         name="steps",
-    )(wave_order, jnp.asarray(weight), wave_rows, table, state, mix, speed, send, fields, partner)
+    )(
+        wave_order, jnp.asarray(weight), wave_order[:, None], jnp.asarray(lat_rows), spectra,
+        vertical_modes, mode_speeds[None], fields,
+    )
 
 
 def solution(mesh):

time: 180 us -> 167 us (0.928)
  Pallas kernels: 170 us -> 160 us
  starting transfers between devices: 2.54 us -> 0 us
    pallas_call x2 -> x1, Pallas kernels: 170 us -> 160 us  [shards(): pl.pallas_call(steps_kernel, out_shape=jax.ShapeDtypeStruct((SLOTS, M, CO...]
    ppermute x1 -> x0, starting transfers between devices: 2.54 us -> none  [shards(): lax.ppermute(fields, 'pert', [(p, (p + 4) % PERT) for p in range(PERT)])]
    unnamed x5 -> x1, local copies, waits for them, and re-layouts: 3.62 us -> 2.72 us
  transfers between devices with their start and end apart: 1 -> 0, of which waited for: 0 -> 0; matrix products, arithmetic and copies ran while one was open for 1% -> 0% of each run, Pallas kernels for 9% -> 0%
where the time goes in v5:
time: 167 us; the launch traced here: 166 us
  Pallas kernels  160 us (96%)
  local copies, waits for them, and re-layouts  4.17 us (2%)
  other arithmetic  2.36 us (1%)
    pallas_call x1, Pallas kernels, shards(): pl.pallas_call(steps_kernel, out_shape=jax.ShapeDtypeStruct((SLOTS, M, CO...  160 us

profile of v5, /device:TPU:1, one launch (start us, length us, event | category | flops | bytes accessed | tf_op | source)
XLA Modules:
  0.0 166.4 jit_solution(15207768887932937813)
XLA Ops:
  0.0 1.5 broadcast_in_dim.12.wave_ref
  1.5 2.4 %maximum_bitcast_fusion.own_ref = bf16[2,15,3,4,960]{4,3,2,1,0:T(4,128)(2,1)} fusion(bf16[2,1,4,15,960]{4,2,1,3,0:T(4,128)(2,1)} %bitcast.4, bf16[2,2,4,15,960]{4,2,3,1,0:T(4,128)(2,1)} %param.11), kind=kLoop, calls=%fused_computation | loop fusion | flops 1382400 | bytes 1382400 | tf_op jit(solution)/shard_map/transpose | solution.py:486
  3.8 159.8 %steps.1 = f32[10,320,128]{2,1,0:T(8,128)} custom-call(s32[320]{0:T(512)} %wave_smem.1, f32[240]{0:T(256)} %constant.4.clone.weight_smem, s32[320,1]{1,0:T(8,128)} %broadcast_in_dim.12.wave_ref, f32[3,256]{1,0:T(4,128)} %constant.5.clone.lat_ref, f32[10,320,128]{2,1,0:T(8,128)} %spectra_ref.1, f32[32,32]{1,0:T(8,128)} %modes_ref.1, f32[1,32]{1,0:T(1,128)} %bitcast.5, ...), custom_call_target="tpu_custom_call" | custom-call | tf_op jit(solution)/shard_map/steps/pallas_call | solution.py:488
  163.7 2.7 %copy.15 = f32[10,320,128]{2,1,0:T(8,128)} copy(f32[10,320,128]{2,1,0:T(8,128)} %steps.1) | data formatting | bytes 3276800

commit v6 on v5

--- a/solution.py
+++ b/solution.py
@@ -152,9 +152,9 @@
 
     ones = jnp.ones((16, 128), F32)
     zeros = jnp.zeros((16, 128), F32)
-    half_way = lax.fori_loop(0, M // 32, block, ((ones, ones), (zeros, zeros), (zeros, zeros)))
+    part_way = lax.fori_loop(0, 3, block, ((ones, ones), (zeros, zeros), (zeros, zeros)))
     between()
-    lax.fori_loop(M // 32, M // 16, block, half_way)
+    lax.fori_loop(3, M // 16, block, part_way)
 
 
 def first_rows(j, w, spectra_ref, scratch, table_ref, state_ref, send_ref):
@@ -201,7 +201,7 @@
     def rows(i, _):
         at = pl.ds(pl.multiple_of(i * 64, 64), 64)
         below = pl.ds(pl.multiple_of(M + i * 64, 64), 64)
-        wave = wave_ref[at, :].astype(F32)
+        wave = wave_ref[at, :]
         x = iota((64, 128), 1).astype(F32)
         angle = angle_of(wave * x)
         turn = angle_of(wave * jnp.full((64, 128), 128.0, F32))
@@ -235,7 +235,7 @@
         return 0
 
     lax.fori_loop(0, SPACE, widen, 0)
-    wave = wave_ref[...].astype(F32)
+    wave = wave_ref[...]
     low = iota((M, COLS), 1) < ROWS
 
     def group(g, _):
@@ -288,9 +288,9 @@
 
 
 def steps_kernel(
-    wave_smem, weight_smem, wave_ref, lat_ref, spectra_ref, modes_ref, speeds_ref, own_ref,
+    wave_smem, weight_smem, lat_ref, spectra_ref, modes_ref, speeds_ref, own_ref,
     out_ref,
-    part, scratch, coefs, table_ref, state_ref, mix_ref, speed_ref, first_ref,
+    part, wave_ref, scratch, coefs, table_ref, state_ref, mix_ref, speed_ref, first_ref,
     traj, synth, analysis, there_0, there_1, grid_0, grid_1, back_0, back_1, second, middle, wide, narrow,
     send_sem, recv_sem, own_sem, ring_send, ring_recv, ring_own, part_send, part_recv,
 ):
@@ -388,6 +388,12 @@
     push(0, 2, 0, late)
     push(0, 1, 1, early)
     push(0, 3, 1, late)
+
+    def wave_row(i, _):
+        wave_ref[pl.ds(i, 1), :] = jnp.full((1, COLS), wave_smem[i], jnp.int32).astype(F32)
+        return 0
+
+    lax.fori_loop(0, M, wave_row, 0)
     crossing[0].wait_recv()
     send_round(0, 1)
     implicit_operators(modes_ref, speeds_ref, mix_ref, speed_ref)
@@ -429,9 +435,11 @@
             for parity in range(2):
                 out_ref[j, pl.ds(parity, HK, stride=2), :] = result[parity * HK : (parity + 1) * HK]
 
+    cuts = (few, 7)
     for step in range(STEPS):
         rows, out = (there_0, grid_0) if step == 0 else (there_1, grid_1)
         back = 2 * step + 1
+        cut = cuts[step]
         for half in range(2):
             arrive(2 * step, half, half, early)
             arrive(2 * step, 2 + half, half, late)
@@ -446,18 +454,18 @@
             if half == 0:
                 push(back, 0, 0)
             else:
-                push(back, 1, 1, early)
-                push(back, 2, 1, late)
+                push(back, 1, 1, pl.ds(0, cut))
+                push(back, 2, 1, pl.ds(cut, SLOTS - cut))
         if step == 0:
             pass_on(1)
         arrive(back, 0, 0)
-        arrive(back, 1, 1, early)
-        for j in range(few):
+        arrive(back, 1, 1, pl.ds(0, cut))
+        for j in range(cut):
             slot(step, j)
         if step == 0:
             push(2, 0, 0, early)
-        arrive(back, 2, 1, late)
-        for j in range(few, SLOTS):
+        arrive(back, 2, 1, pl.ds(cut, SLOTS - cut))
+        for j in range(cut, SLOTS):
             slot(step, j)
         if step == 0:
             push(2, 2, 0, late)
@@ -467,10 +475,10 @@
         for half in range(2):
             drain(e, half, half, early)
             drain(e, 2 + half, half, late)
-    for e in (1, 3):
+    for e, cut in ((1, cuts[0]), (3, cuts[1])):
         drain(e, 0, 0)
-        drain(e, 1, 1, early)
-        drain(e, 2, 1, late)
+        drain(e, 1, 1, pl.ds(0, cut))
+        drain(e, 2, 1, pl.ds(cut, SLOTS - cut))
     for c in list(rings.values()) + passed + crossing:
         c.wait_send()
 
@@ -488,10 +496,11 @@
     return pl.pallas_call(
         steps_kernel,
         out_shape=jax.ShapeDtypeStruct((SLOTS, M, COLS), F32),
-        in_specs=[SMEM] * 2 + [VMEM] * 5 + [ANY],
+        in_specs=[SMEM] * 2 + [VMEM] * 4 + [ANY],
         out_specs=VMEM,
         scratch_shapes=[
             pltpu.VMEM(fields.shape, BF16),
+            pltpu.VMEM((M, COLS), F32),
             pltpu.VMEM((2, 16 * APART, 128), F32),
             pltpu.VMEM((2, 3, 16, 128), F32),
             pltpu.VMEM((SLOTS, M, HALF), BF16),
@@ -515,7 +524,7 @@
         ),
         name="steps",
     )(
-        wave_order, jnp.asarray(weight), wave_order[:, None], jnp.asarray(lat_rows), spectra,
+        wave_order, jnp.asarray(weight), jnp.asarray(lat_rows), spectra,
         vertical_modes, mode_speeds[None], fields,
     )
 

time: 167 us -> 161 us (0.964)
  Pallas kernels: 160 us -> 155 us
    pallas_call x1, Pallas kernels: 160 us -> 155 us  [shards(): pl.pallas_call(steps_kernel, out_shape=jax.ShapeDtypeStruct((SLOTS, M, CO...]
where the time goes in v6:
time: 161 us; the launch traced here: 160 us
  Pallas kernels  155 us (96%)
  local copies, waits for them, and re-layouts  2.72 us (2%)
  other arithmetic  2.36 us (1%)
    pallas_call x1, Pallas kernels, shards(): pl.pallas_call(steps_kernel, out_shape=jax.ShapeDtypeStruct((SLOTS, M, CO...  155 us

profile of v6, /device:TPU:1, one launch (start us, length us, event | category | flops | bytes accessed | tf_op | source)
XLA Modules:
  0.0 160.4 jit_solution(2185256566267653510)
XLA Ops:
  0.0 2.4 %maximum_bitcast_fusion.own_ref = bf16[2,15,3,4,960]{4,3,2,1,0:T(4,128)(2,1)} fusion(bf16[2,1,4,15,960]{4,2,1,3,0:T(4,128)(2,1)} %bitcast.4, bf16[2,2,4,15,960]{4,2,3,1,0:T(4,128)(2,1)} %param.11), kind=kLoop, calls=%fused_computation | loop fusion | flops 1382400 | bytes 1382400 | tf_op jit(solution)/shard_map/transpose | solution.py:494
  2.4 155.3 %steps.1 = f32[10,320,128]{2,1,0:T(8,128)} custom-call(s32[320]{0:T(512)} %wave_smem.1, f32[240]{0:T(256)} %constant.4.clone.weight_smem, f32[3,256]{1,0:T(4,128)} %constant.5.clone.lat_ref, f32[10,320,128]{2,1,0:T(8,128)} %spectra_ref.1, f32[32,32]{1,0:T(8,128)} %modes_ref.1, f32[1,32]{1,0:T(1,128)} %bitcast.5, ...), custom_call_target="tpu_custom_call" | custom-call | tf_op jit(solution)/shard_map/steps/pallas_call | solution.py:496
  157.7 2.7 %copy.13 = f32[10,320,128]{2,1,0:T(8,128)} copy(f32[10,320,128]{2,1,0:T(8,128)} %steps.1) | data formatting | bytes 3276800

commit v7 on v6

--- a/solution.py
+++ b/solution.py
@@ -520,7 +520,7 @@
         + [pltpu.SemaphoreType.DMA((STEPS, 2))]
         + [pltpu.SemaphoreType.DMA((STEPS,))] * 2,
         compiler_params=pltpu.CompilerParams(
-            collective_id=1, has_side_effects=True, vmem_limit_bytes=60 * 2**20
+            collective_id=1, has_side_effects=True, vmem_limit_bytes=46 * 2**20
         ),
         name="steps",
     )(

time: 161 us -> 163 us (1.012); the launches traced: 160 us -> 161 us
  local copies, waits for them, and re-layouts: 2.72 us -> 6.01 us
  Pallas kernels: 155 us -> 153 us
    unnamed x1 -> x13, local copies, waits for them, and re-layouts: 2.72 us -> 6.01 us
    pallas_call x1, Pallas kernels: 155 us -> 153 us  [shards(): pl.pallas_call(steps_kernel, out_shape=jax.ShapeDtypeStruct((SLOTS, M, CO...]
where the time goes in v7:
time: 163 us; the launch traced here: 161 us
  Pallas kernels  153 us (94%)
  local copies, waits for them, and re-layouts  6.01 us (4%)
    pallas_call x1, Pallas kernels, shards(): pl.pallas_call(steps_kernel, out_shape=jax.ShapeDtypeStruct((SLOTS, M, CO...  153 us
    unnamed x13, local copies, waits for them, and re-layouts  6.01 us

profile of v7, /device:TPU:1, one launch (start us, length us, event | category | flops | bytes accessed | tf_op | source)
XLA Modules:
  0.0 160.6 jit_solution(13198233963128348011)
XLA Ops:
  0.0 1.5 maximum_bitcast_fusion.own_ref
  1.5 0.0 copy-start
  1.5 1.4 copy-done
  2.9 0.0 copy-start.1
  2.9 0.7 copy-done.1
  3.6 0.0 copy-start.2
  3.7 0.7 copy-done.2
  4.3 0.0 copy-start.3
  4.3 0.7 copy-done.3
  5.0 0.0 copy-start.4
  5.0 0.7 copy-done.4
  5.7 0.0 copy-start.5
  5.7 0.7 copy-done.5
  6.4 153.1 %steps.1 = f32[10,320,128]{2,1,0:T(8,128)S(1)} custom-call(s32[320]{0:T(512)S(1)} %copy-done.3, f32[240]{0:T(256)S(1)} %copy-done.4, f32[3,256]{1,0:T(4,128)S(1)} %copy-done.2, f32[10,320,128]{2,1,0:T(8,128)S(1)} %copy-done, f32[32,32]{1,0:T(8,128)S(1)} %copy-done.1, f32[1,32]{1,0:T(1,128)S(1)} %bitcast.4, ...), custom_call_target="tpu_custom_call" | custom-call | tf_op jit(solution)/shard_map/steps/pallas_call | solution.py:496
  159.5 1.2 copy.13
Async XLA Ops:
  1.5 1.4 copy-start
  2.9 0.7 copy-start.1
  3.6 0.7 copy-start.2
  4.3 0.7 copy-start.3
  5.0 0.7 copy-start.4
  5.7 0.7 copy-start.5

commit v8 on v6

--- a/solution.py
+++ b/solution.py
@@ -152,9 +152,9 @@
 
     ones = jnp.ones((16, 128), F32)
     zeros = jnp.zeros((16, 128), F32)
-    part_way = lax.fori_loop(0, 3, block, ((ones, ones), (zeros, zeros), (zeros, zeros)))
+    part_way = lax.fori_loop(0, 1, block, ((ones, ones), (zeros, zeros), (zeros, zeros)))
     between()
-    lax.fori_loop(3, M // 16, block, part_way)
+    lax.fori_loop(1, M // 16, block, part_way)
 
 
 def first_rows(j, w, spectra_ref, scratch, table_ref, state_ref, send_ref):

time: 161 us -> 161 us (level)
  no operation moved by 1% of the time
where the time goes in v8:
time: 161 us; the launch traced here: 160 us
  Pallas kernels  155 us (96%)
  local copies, waits for them, and re-layouts  2.72 us (2%)
  other arithmetic  2.36 us (1%)
    pallas_call x1, Pallas kernels, shards(): pl.pallas_call(steps_kernel, out_shape=jax.ShapeDtypeStruct((SLOTS, M, CO...  155 us

profile of v8, /device:TPU:1, one launch (start us, length us, event | category | flops | bytes accessed | tf_op | source)
XLA Modules:
  0.0 160.4 jit_solution(15642479757377353010)
XLA Ops:
  0.0 2.4 %maximum_bitcast_fusion.own_ref = bf16[2,15,3,4,960]{4,3,2,1,0:T(4,128)(2,1)} fusion(bf16[2,1,4,15,960]{4,2,1,3,0:T(4,128)(2,1)} %bitcast.4, bf16[2,2,4,15,960]{4,2,3,1,0:T(4,128)(2,1)} %param.11), kind=kLoop, calls=%fused_computation | loop fusion | flops 1382400 | bytes 1382400 | tf_op jit(solution)/shard_map/transpose | solution.py:494
  2.4 155.3 %steps.1 = f32[10,320,128]{2,1,0:T(8,128)} custom-call(s32[320]{0:T(512)} %wave_smem.1, f32[240]{0:T(256)} %constant.4.clone.weight_smem, f32[3,256]{1,0:T(4,128)} %constant.5.clone.lat_ref, f32[10,320,128]{2,1,0:T(8,128)} %spectra_ref.1, f32[32,32]{1,0:T(8,128)} %modes_ref.1, f32[1,32]{1,0:T(1,128)} %bitcast.5, ...), custom_call_target="tpu_custom_call" | custom-call | tf_op jit(solution)/shard_map/steps/pallas_call | solution.py:496
  157.7 2.7 %copy.13 = f32[10,320,128]{2,1,0:T(8,128)} copy(f32[10,320,128]{2,1,0:T(8,128)} %steps.1) | data formatting | bytes 3276800
